TPU v7x, 128 devices: a whole 4x4x4 slice. The times are simulated.
128 devices in a mesh: ctx: 32 (over z, x, core), head: 4 (over y).
Axes of the slice: x: 4, y: 4, z: 4, core: 2. Of those that a mesh axis runs over, the one named last changes fastest.
Arguments:
- queries: bfloat16 [16384, 4096], P('ctx', 'head'), may hold values from -8 to 8
- keys: bfloat16 [16384, 512], P('ctx', 'head'), may hold values from -8 to 8
- values: bfloat16 [16384, 512], P('ctx', 'head'), may hold values from -6 to 6
- distances: int32 [4, 3], P('head'), may hold values from 1 to 31, as said below
- out_weight: bfloat16 [4096, 2048], P('head'), may hold values from -0.09375 to 0.09375
- residual: bfloat16 [16384, 2048], P(('ctx', 'head')), may hold values from -6 to 6
- norm_gain: float32 [2048], replicated, may hold values from 0.25 to 1.75
- expert_gate_up: bfloat16 [128, 2048, 1536], P(('ctx', 'head')), may hold values from -0.125 to 0.125
- expert_down: bfloat16 [128, 768, 2048], P(('ctx', 'head')), may hold values from -0.21875 to 0.21875
- routes: int32 [16384, 8], P(('ctx', 'head')), may hold values from 0 to 127, all different within a row; in each aligned block of 128 rows (0 to 127, 128 to 255, ...) at most 16 rows name the same one
- route_weights: float32 [16384, 8], P(('ctx', 'head')), may hold values from 0.05 to 0.5
Outputs:
- attended: bfloat16 [16384, 2048], P(('ctx', 'head'))
- moe_out: bfloat16 [16384, 2048], P(('ctx', 'head'))
Inputs may be any that keep to these rules, and one draw needn't show every extreme that they name: Each row holds 3 different distances; some row holds the distance 16384 // 1024. `routes`: among the 128 rows of one device, no expert is named by more than 16 rows.
All inputs are finite; a program needn't handle non-finite values.
Results may differ from a plain program's by a relative error of at most 0.01.
Values may be sent and summed in bfloat16 or wider, within the bound.
No kernel may reach another device: no remote copies, remote signals or barrier semaphores. Data moves between devices by JAX's collectives and lax.ppermute only.
A program may use at most 128 MiB of HBM per device.

v0:
```python
import math

import jax
import jax.numpy as jnp
from jax import lax
from jax.sharding import PartitionSpec as P

HD = 128
FFE = 768
TOP = 8
EXP_DEV = 1
BLK = 128
DIST = 3


def expert_rows(arrived, expert_gate_up, expert_down, sources):
    width = arrived.shape[2]
    grid = arrived.reshape(sources, EXP_DEV, arrived.shape[1], width)
    projected = jnp.einsum(
        "sekd,edf->eskf", grid, expert_gate_up, preferred_element_type=jnp.float32
    )
    hidden = (jax.nn.silu(projected[..., :FFE]) * projected[..., FFE:]).astype(jnp.bfloat16)
    output = jnp.einsum("eskf,efd->sekd", hidden, expert_down, preferred_element_type=jnp.float32)
    return output.astype(jnp.bfloat16).reshape(arrived.shape)


def body(
    queries,
    keys,
    values,
    distances,
    out_weight,
    residual,
    norm_gain,
    expert_gate_up,
    expert_down,
    routes,
    route_weights,
):
    length = queries.shape[0]
    groups = queries.shape[1] // HD
    blocks = length // BLK
    scale = 1.0 / math.sqrt(HD)
    wanted = distances[0]
    source = lax.axis_index("ctx") - wanted
    usable = source >= 0
    packed = jnp.concatenate([keys, values], axis=1)
    everything = lax.all_gather(packed, "ctx", axis=0, tiled=True)
    offsets = jnp.maximum(source, 0) * length
    fetched = jnp.stack(
        [
            lax.dynamic_slice_in_dim(everything, offsets[slot_index], length, 0)
            for slot_index in range(DIST)
        ]
    )
    query = queries.reshape(length, groups, HD)
    causal = jnp.arange(length)[:, None] >= jnp.arange(length)[None, :]
    local = jnp.einsum("tgd,ud->gtu", query, keys, preferred_element_type=jnp.float32) * scale
    local = jnp.where(causal[None], local, -jnp.inf)
    far_keys = fetched[:, :, :HD].reshape(DIST, blocks, BLK, HD)
    far_values = fetched[:, :, HD:].reshape(DIST, blocks, BLK, HD)
    query_blocks = queries.reshape(blocks, BLK, groups, HD)
    remote = (
        jnp.einsum("bqgd,jbud->gjbqu", query_blocks, far_keys, preferred_element_type=jnp.float32)
        * scale
    )
    remote = jnp.where(usable[None, :, None, None, None], remote, -jnp.inf)
    highest = jnp.maximum(local.max(-1), remote.max(axis=(1, 4)).reshape(groups, length))
    near_weight = jnp.exp(local - highest[:, :, None])
    far_weight = jnp.exp(remote - highest.reshape(groups, blocks, BLK)[:, None, :, :, None])
    denominator = near_weight.sum(-1) + far_weight.sum(axis=(1, 4)).reshape(groups, length)
    mixed = jnp.einsum(
        "gtu,ud->tgd", near_weight.astype(jnp.bfloat16), values, preferred_element_type=jnp.float32
    )
    far_mixed = jnp.einsum(
        "gjbqu,jbud->bqgd",
        far_weight.astype(jnp.bfloat16),
        far_values,
        preferred_element_type=jnp.float32,
    )
    mixed = mixed + far_mixed.reshape(length, groups, HD)
    attention = (
        (mixed / jnp.transpose(denominator)[:, :, None])
        .astype(jnp.bfloat16)
        .reshape(length, groups * HD)
    )
    summed = lax.psum_scatter(
        jnp.dot(attention, out_weight, preferred_element_type=jnp.float32),
        "head",
        scatter_dimension=0,
        tiled=True,
    )
    attended = (residual.astype(jnp.float32) + summed).astype(jnp.bfloat16)
    widened = attended.astype(jnp.float32)
    inverse = lax.rsqrt(jnp.mean(widened * widened, axis=-1, keepdims=True) + 1e-06)
    normed = (widened * inverse * norm_gain).astype(jnp.bfloat16)
    local_rows = normed.shape[0]
    width = normed.shape[1]
    devices = lax.axis_size(("ctx", "head"))
    experts = devices * EXP_DEV
    capacity = max(2, 2 * local_rows * TOP // experts)
    flat_experts = routes.reshape(local_rows * TOP)
    onehot = (flat_experts[:, None] == jnp.arange(experts, dtype=jnp.int32)[None, :]).astype(
        jnp.int32
    )
    places = jnp.sum(jnp.cumsum(onehot, axis=0) * onehot, axis=1) - 1
    owners = jnp.arange(local_rows * TOP, dtype=jnp.int32) // TOP
    outgoing = (
        jnp.zeros((experts, capacity, width), jnp.bfloat16)
        .at[flat_experts, places]
        .set(normed[owners])
    )
    answered = expert_rows(
        lax.all_to_all(outgoing, ("ctx", "head"), split_axis=0, concat_axis=0, tiled=True),
        expert_gate_up,
        expert_down,
        devices,
    )
    returned = lax.all_to_all(answered, ("ctx", "head"), split_axis=0, concat_axis=0, tiled=True)
    picked = returned[flat_experts, places].astype(jnp.float32)
    weighted = route_weights.reshape(local_rows * TOP)[:, None] * picked
    moe_out = weighted.reshape(local_rows, TOP, width).sum(axis=1).astype(jnp.bfloat16)
    return (attended, moe_out)


def solution(mesh):
    return jax.shard_map(
        body,
        mesh=mesh,
        in_specs=(
            P("ctx", "head"),
            P("ctx", "head"),
            P("ctx", "head"),
            P("head", None),
            P("head", None),
            P(("ctx", "head"), None),
            P(),
            P(("ctx", "head"), None, None),
            P(("ctx", "head"), None, None),
            P(("ctx", "head"), None),
            P(("ctx", "head"), None),
        ),
        out_specs=(P(("ctx", "head"), None), P(("ctx", "head"), None)),
        check_vma=False,
    )
```

profile of v0, /device:TPU:1, one launch (start us, length us, event | category | flops | bytes accessed | tf_op | source)
XLA Modules:
  0.0 478.4 jit_solution(17237951945180817351)
XLA Ops:
  7.2 1.9 pad_maximum_fusion.1
  9.2 0.7 maximum_multiply_fusion
  9.8 0.7 fusion.53
  14.4 2.6 copy.69
  19.0 0.7 compare_bitcast_fusion
  19.7 2.3 bitcast_bitcast_fusion
  21.9 5.9 %fusion.8 = (f32[8,512]{1,0:T(8,128)S(1)}, f32[512,512,8]{1,0,2:T(8,128)}) fusion(pred[512,512]{0,1:T(8,128)(4,1)S(1)} %iota_compare_fusion, bf16[512,128]{1,0:T(8,128)(2,1)} %param.12, bf16[512,1024]{1,0:T(8,128)(2,1)} %param.11), kind=kOutput, calls=%fused_computation.12 | convolution fusion | flops 543158272 | bytes 9846784 | tf_op jit(solution)/shard_map/tgd,ud->gtu/dot_general | solution.py:58
  27.9 39.7 %all-gather.2.cloned.1.call-done = bf16[16384,256]{1,0:T(8,128)(2,1)} async-done(((bf16[512,256]{1,0:T(8,128)(2,1)}), bf16[16384,256]{1,0:T(8,128)(2,1)}) %all-gather.2.cloned.1.call-update) | async-done | bytes 8388624 | tf_op jit(solution)/shard_map/all_gather | solution.py:48
  67.5 1.4 dynamic-slice_bitcast_fusion.2
  69.2 2.2 bitcast_reduce_fusion
  71.4 2.2 fusion.12
  73.6 2.5 fusion.27
  76.1 3.2 copy.44
  79.3 3.1 reshape.226
  82.4 5.3 %fusion.3 = f32[8,512]{1,0:T(8,128)S(1)} fusion(f32[512,512,8]{1,0,2:T(8,128)} %get-tuple-element.22, f32[8,512]{1,0:T(8,128)S(1)} %bitcast_maximum_fusion.1, pred[512,512]{0,1:T(8,128)(4,1)S(1)} %iota_compare_fusion), kind=kLoop, calls=%fused_computation.9 | loop fusion | flops 8384512 | bytes 8683520 | tf_op jit(solution)/shard_map/reduce_sum | solution.py:71
  87.7 5.7 %fusion.26 = bf16[512,8,128]{0,2,1:T(8,128)(2,1)S(1)} fusion(f32[512,8,128]{0,2,1:T(8,128)S(1)} %copy-done.4, f32[512,512,8]{1,0,2:T(8,128)} %get-tuple-element.22, f32[8,512]{1,0:T(8,128)S(1)} %bitcast_maximum_fusion.1, pred[512,512]{0,1:T(8,128)(4,1)S(1)} %iota_compare_fusion, f32[512,8]{0,1:T(8,128)S(1)} %fusion.48, bf16[512,128]{1,0:T(8,128)(2,1)S(1)} %copy-done.5), kind=kOutput, calls=%fused_computation.34 | convolution fusion | flops 546832384 | bytes 11960320 | tf_op jit(solution)/shard_map/gtu,ud->tgd/dot_general | solution.py:72
  93.4 4.4 fusion.54
  98.6 0.8 copy-done.2
  99.4 1.1 broadcast_add_fusion
  101.2 42.7 %reduce-scatter.2.cloned.1.call-done = f32[128,2048]{1,0:T(8,128)} async-done(((f32[512,2048]{1,0:T(8,128)}), f32[128,2048]{1,0:T(8,128)}) %reduce-scatter.2.cloned.1.call-update) | async-done | bytes 1048592 | tf_op jit(solution)/shard_map/reduce_scatter | solution.py:87
  143.9 1.6 fusion.32
  145.5 0.8 copy-done.3
  146.3 1.0 fusion.34
  147.3 26.0 %scatter_custom_fusion = bf16[2048,2048]{1,0:T(8,128)(2,1)} fusion(s32[1024]{0:T(1024)S(1)} %get-tuple-element.24, bf16[128,2048]{1,0:T(8,128)(2,1)} %fusion.34, s32[1024]{0:T(1024)S(1)} %get-tuple-element.23, bf16[]{:T(256)} %constant.49.clone.1), kind=kCustom, calls=%fused_computation.23 | custom fusion | bytes 8389120
  173.3 106.1 %all_to_all.10 = bf16[128,16,2048]{2,1,0:T(8,128)(2,1)S(1)} all-to-all(bf16[128,16,2048]{2,1,0:T(8,128)(2,1)} %bitcast.117), channel_id=1, replica_groups=mesh['ctx'=32,'head'=4] {'ctx','head'}, dimensions={0} | all-to-all | bytes 16777216 | tf_op jit(solution)/shard_map/all_to_all | solution.py:114
  279.4 35.8 %fusion.5 = f32[1,128,16,1536]{3,1,2,0:T(8,128)S(1)} fusion(bf16[128,16,2048]{2,1,0:T(8,128)(2,1)S(1)} %all_to_all.10, bf16[1,2048,1536]{2,1,0:T(8,128)(2,1)} %param.18), kind=kOutput, calls=%fused_computation.11 | convolution fusion | flops 12884901888 | bytes 27262976 | tf_op jit(solution)/shard_map/sekd,edf->eskf/dot_general | solution.py:19
  315.2 8.9 %convolution_convert_fusion = bf16[128,16,2048]{2,0,1:T(8,128)(2,1)} fusion(bf16[1,768,2048]{2,1,0:T(8,128)(2,1)S(1)} %copy-done, f32[1,128,16,1536]{3,1,2,0:T(8,128)S(1)} %fusion.5), kind=kOutput, calls=%fused_computation.20 | convolution fusion | flops 6456082432 | bytes 24117248 | tf_op jit(solution)/shard_map/eskf,efd->sekd/dot_general | solution.py:23
  324.2 11.2 %copy.52 = bf16[128,16,2048]{2,1,0:T(8,128)(2,1)} copy(bf16[128,16,2048]{2,0,1:T(8,128)(2,1)} %convolution_convert_fusion) | data formatting | bytes 16777216 | tf_op jit(solution)/shard_map/convert_element_type | solution.py:24
  335.4 5.2 %all-to-all-start.1 = ((bf16[128,16,2048]{2,1,0:T(8,128)(2,1)}), bf16[128,16,2048]{2,1,0:T(8,128)(2,1)}, u32[]{:S(2)}, u32[]{:S(2)}) async-start(bf16[128,16,2048]{2,1,0:T(8,128)(2,1)} %copy.52), calls=%async_computation.2 | async-start | bytes 16777216 | tf_op jit(solution)/shard_map/all_to_all | solution.py:119
  340.7 97.5 %all-to-all-done.1 = bf16[128,16,2048]{2,1,0:T(8,128)(2,1)} async-done(((bf16[128,16,2048]{2,1,0:T(8,128)(2,1)}), bf16[128,16,2048]{2,1,0:T(8,128)(2,1)}, u32[]{:S(2)}, u32[]{:S(2)}) %all-to-all-start.1) | async-done | bytes 8388640 | tf_op jit(solution)/shard_map/all_to_all | solution.py:119
  438.2 25.6 %gather_fusion = bf16[1024,2048]{1,0:T(8,128)(2,1)} fusion(bf16[128,16,2048]{2,1,0:T(8,128)(2,1)} %all-to-all-done.1, s32[1024]{0:T(1024)S(1)} %bitcast.116), kind=kCustom, calls=%fused_computation.1 | custom fusion | bytes 8396800 | tf_op jit(solution)/shard_map/gather | solution.py:120
  463.8 7.3 %fusion = bf16[128,2048]{1,0:T(8,128)(2,1)} fusion(bf16[1024,2048]{1,0:T(8,128)(2,1)} %gather_fusion, f32[128,8]{1,0:T(8,128)S(1)} %copy.45), kind=kLoop, calls=%fused_computation.4 | loop fusion | flops 6029312 | bytes 4722688 | tf_op jit(solution)/shard_map/reduce_sum | solution.py:122
  (51 shorter events, 2.0 us)
Async XLA Ops:
  7.2 308.0 %copy-start = (bf16[1,768,2048]{2,1,0:T(8,128)(2,1)S(1)}, bf16[1,768,2048]{2,1,0:T(8,128)(2,1)}, u32[]{:S(2)}) copy-start(bf16[1,768,2048]{2,1,0:T(8,128)(2,1)} %param.19) | copy-start | bytes 9437188
  7.2 60.4 %all-gather.2.cloned.1.call-start = ((), (), s32[]{:S(2)}) async-start(), calls=%async_computation.3 | async-start | bytes 8650752 | tf_op jit(solution)/shard_map/all_gather | solution.py:48
  9.1 134.8 %reduce-scatter.2.cloned.1.call-start = ((), (), s32[]{:S(2)}) async-start(), calls=%async_computation.4 | async-start | bytes 5242880 | tf_op jit(solution)/shard_map/reduce_scatter | solution.py:87
  79.3 8.4 %copy-start.5 = (bf16[512,128]{1,0:T(8,128)(2,1)S(1)}, bf16[512,128]{1,0:T(8,128)(2,1)}, u32[]{:S(2)}) copy-start(bf16[512,128]{1,0:T(8,128)(2,1)} %param.13) | copy-start | bytes 393220
  82.4 5.3 %copy-start.6 = (f32[8,4,128]{2,0,1:T(8,128)S(1)}, f32[8,4,128]{2,0,1:T(8,128)}, u32[]{:S(2)}) copy-start(f32[8,4,128]{2,0,1:T(8,128)} %get-tuple-element.9) | copy-start | bytes 49156
  82.4 5.3 %copy-start.4 = (f32[512,8,128]{0,2,1:T(8,128)S(1)}, f32[512,8,128]{0,2,1:T(8,128)}, u32[]{:S(2)}) copy-start(f32[512,8,128]{0,2,1:T(8,128)} %reshape.226) | copy-start | bytes 6291460
  87.7 5.7 %copy-start.1 = (bf16[1024,2048]{1,0:T(8,128)(2,1)S(1)}, bf16[1024,2048]{1,0:T(8,128)(2,1)}, u32[]{:S(2)}) copy-start(bf16[1024,2048]{1,0:T(8,128)(2,1)} %param.15) | copy-start | bytes 12582916
  93.4 4.4 copy-start.8
  97.8 3.2 copy-start.11
  97.8 3.3 copy-start.10
  97.8 48.5 %copy-start.7 = (f32[2048]{0:T(1024)S(1)}, f32[2048]{0:T(1024)}, u32[]{:S(2)}) copy-start(f32[2048]{0:T(1024)} %param.17) | copy-start | bytes 24580
  98.5 0.8 copy-start.2
  145.5 0.8 copy-start.3
  335.4 5.3 %copy-start.9 = (f32[128,8]{0,1:T(8,128)S(1)}, f32[128,8]{0,1:T(8,128)}, u32[]{:S(2)}) copy-start(f32[128,8]{0,1:T(8,128)} %param.21) | copy-start | bytes 12292
  335.4 102.8 %all-to-all-start.1 = ((bf16[128,16,2048]{2,1,0:T(8,128)(2,1)}), bf16[128,16,2048]{2,1,0:T(8,128)(2,1)}, u32[]{:S(2)}, u32[]{:S(2)}) async-start(bf16[128,16,2048]{2,1,0:T(8,128)(2,1)} %copy.52), calls=%async_computation.2 | async-start | bytes 16777216 | tf_op jit(solution)/shard_map/all_to_all | solution.py:119
Sparse Core Ops, SparseCore 0:
  10.8 56.6 all-gather.1
  98.0 45.8 reduce-scatter.1
where the time goes:
time: 488 us; the launch traced here: 478 us
  waiting for transfers between devices  180 us (37%)
  blocking collectives  106 us (22%)
  local copies, waits for them, and re-layouts  78.4 us (16%)
  matrix products  65.5 us (13%)
  other arithmetic  22.6 us (5%)
  between operations  20.6 us (4%)
  starting transfers between devices  5.32 us (1%)
    all_to_all x1, blocking collectives, body(): lax.all_to_all(outgoing, ('ctx', 'head'), split_axis=0, concat_axis=0, ti...  106 us
    all_to_all x1, waiting for transfers between devices, body(): lax.all_to_all(answered, ('ctx', 'head'), split_axis=0, concat_axis=0, ti...  97.5 us
    reduce_scatter x1, waiting for transfers between devices, body(): lax.psum_scatter(jnp.dot(attention, out_weight, preferred_element_type=jn...  42.7 us
    all_gather x1, waiting for transfers between devices, body(): everything = lax.all_gather(packed, 'ctx', axis=0, tiled=True)  39.7 us
    dot_general x1, matrix products, expert_rows(): jnp.einsum('sekd,edf->eskf', grid, expert_gate_up, preferred_element_type...  35.8 us
    unnamed x28, local copies, waits for them, and re-layouts  30.4 us
    gather x1, local copies, waits for them, and re-layouts, body(): picked = returned[flat_experts, places].astype(jnp.float32)  25.6 us
    convert_element_type x1, local copies, waits for them, and re-layouts, expert_rows(): return output.astype(jnp.bfloat16).reshape(arrived.shape)  11.2 us
  transfers between devices with their start and end apart: 3, of which 3 were waited for; matrix products, arithmetic and copies ran while one was open for 3% of the time, Pallas kernels for 0%

commit v1 on v0

v1 whole, which is shorter than its diff:
```python
import functools
import math

import jax
import jax.numpy as jnp
from jax import lax
from jax.experimental import pallas as pl
from jax.experimental.pallas import tpu as pltpu
from jax.sharding import PartitionSpec as P

HD = 128
FFE = 768
TOP = 8
BLK = 128
DIST = 3
CAP = 16
CHUNKS = 2
ALL = ("ctx", "head")
BF16 = jnp.bfloat16
F32 = jnp.float32
NT = (((1,), (1,)), ((), ()))
TN = (((0,), (0,)), ((), ()))
EXPONENT = math.log2(math.e) / math.sqrt(HD)
VMEM_LIMIT = 56 * 1024 * 1024


def params(steps=1):
    return pltpu.CompilerParams(
        dimension_semantics=("arbitrary",) * steps, vmem_limit_bytes=VMEM_LIMIT
    )


def attention_kernel(usable, q_ref, k_ref, v_ref, fk_ref, fv_ref, w_ref, out_ref, mixed_ref):
    block = pl.program_id(0)
    heads = q_ref.shape[1] // HD
    blocks = k_ref.shape[0] // BLK

    def attend(at):
        near = at * BLK
        wide = near + BLK
        keys = jnp.concatenate([k_ref[:wide]] + [fk_ref[j] for j in range(DIST)], axis=0)
        values = jnp.concatenate([v_ref[:wide]] + [fv_ref[j] for j in range(DIST)], axis=0)
        rows = lax.broadcasted_iota(jnp.int32, (BLK, BLK), 0)
        columns = lax.broadcasted_iota(jnp.int32, (BLK, BLK), 1)
        parts = [jnp.zeros((BLK, near), F32)] if at else []
        parts.append(jnp.where(rows >= columns, 0.0, -jnp.inf))
        for j in range(DIST):
            parts.append(jnp.full((BLK, BLK), jnp.where(usable[j] > 0, 0.0, -jnp.inf), F32))
        bias = jnp.concatenate(parts, axis=1)
        for n in range(heads):
            query = q_ref[:, n * HD : (n + 1) * HD]
            score = lax.dot_general(query, keys, NT, preferred_element_type=F32) + bias
            highest = jnp.max(score, axis=1, keepdims=True)
            weight = jnp.exp2((score - highest) * EXPONENT)
            denominator = jnp.sum(weight, axis=1, keepdims=True)
            mixed = jnp.dot(weight.astype(BF16), values, preferred_element_type=F32)
            mixed_ref[:, n * HD : (n + 1) * HD] = (mixed / denominator).astype(BF16)

    for at in range(blocks):
        pl.when(block == at)(functools.partial(attend, at))
    out_ref[...] = jnp.dot(mixed_ref[...], w_ref[...], preferred_element_type=F32).astype(BF16)


def attention(usable, queries, keys, values, far_keys, far_values, out_weight):
    length, wide = queries.shape
    width = out_weight.shape[1]
    whole = lambda shape: pl.BlockSpec(
        shape, lambda b, u: (0,) * len(shape), pipeline_mode=pl.Buffered(1)
    )
    return pl.pallas_call(
        attention_kernel,
        grid_spec=pltpu.PrefetchScalarGridSpec(
            num_scalar_prefetch=1,
            grid=(length // BLK,),
            in_specs=[
                pl.BlockSpec((BLK, wide), lambda b, u: (b, 0)),
                whole(keys.shape),
                whole(values.shape),
                pl.BlockSpec((DIST, BLK, HD), lambda b, u: (0, b, 0)),
                pl.BlockSpec((DIST, BLK, HD), lambda b, u: (0, b, 0)),
                whole(out_weight.shape),
            ],
            out_specs=pl.BlockSpec((BLK, width), lambda b, u: (b, 0)),
            scratch_shapes=[pltpu.VMEM((BLK, wide), BF16)],
        ),
        out_shape=jax.ShapeDtypeStruct((length, width), BF16),
        compiler_params=params(),
        name="attention",
    )(usable, queries, keys, values, far_keys, far_values, out_weight)


def tables_kernel(routes_ref, weights_ref, send_ref, high_ref, low_ref):
    top, tokens = routes_ref.shape
    experts = send_ref.shape[1]
    chunks, slots = send_ref.shape[0], send_ref.shape[2]
    names = lax.broadcasted_iota(jnp.int32, (experts, tokens), 0)
    chosen = jnp.zeros((experts, tokens), F32)
    weight = jnp.zeros((experts, tokens), F32)
    for k in range(top):
        here = routes_ref[k : k + 1, :] == names
        chosen = jnp.where(here, 1.0, chosen)
        weight = jnp.where(here, weights_ref[k : k + 1, :], weight)
    before = (
        lax.broadcasted_iota(jnp.int32, (tokens, tokens), 0)
        < lax.broadcasted_iota(jnp.int32, (tokens, tokens), 1)
    ).astype(BF16)
    place = jnp.dot(chosen.astype(BF16), before, preferred_element_type=F32)
    place = jnp.where(chosen > 0.0, place, -1.0)
    high = weight.astype(BF16).astype(F32)
    low = weight - high
    for c in range(chunks):
        for s in range(slots):
            here = place == float(c * slots + s)
            send_ref[c, :, s, :] = jnp.where(here, 1.0, 0.0)
            high_ref[c, :, s, :] = jnp.where(here, high, 0.0)
            low_ref[c, :, s, :] = jnp.where(here, low, 0.0)


def tables(routes, route_weights, experts):
    tokens = routes.shape[0]
    shape = jax.ShapeDtypeStruct((CHUNKS, experts, CAP // CHUNKS, tokens), F32)
    send, high, low = pl.pallas_call(
        tables_kernel, out_shape=(shape,) * 3, compiler_params=params(0), name="tables"
    )(routes.T, route_weights.T)
    rows = experts * CAP // CHUNKS
    flat = lambda a: a.reshape(CHUNKS, rows, tokens).astype(BF16)
    return flat(send), jnp.concatenate([flat(high), flat(low)], axis=2)


def norm_kernel(parts_ref, residual_ref, gain_ref, send_ref, attended_ref, normed_ref, out_ref):
    @pl.when(pl.program_id(0) == 0)
    def _():
        total = residual_ref[...].astype(F32)
        for i in range(parts_ref.shape[0]):
            total = total + parts_ref[i].astype(F32)
        attended = total.astype(BF16)
        attended_ref[...] = attended
        wide = attended.astype(F32)
        inverse = lax.rsqrt(jnp.mean(wide * wide, axis=1, keepdims=True) + 1e-06)
        normed_ref[...] = (wide * inverse * gain_ref[...]).astype(BF16)

    out_ref[...] = jnp.dot(send_ref[...], normed_ref[...], preferred_element_type=F32).astype(BF16)


def norm_dispatch(parts, residual, gain, send):
    tokens, width = residual.shape
    rows = send.shape[0]
    step = 256
    whole = lambda shape: pl.BlockSpec(shape, lambda i: (0,) * len(shape))
    return pl.pallas_call(
        norm_kernel,
        grid=(rows // step,),
        in_specs=[
            whole(parts.shape),
            whole(residual.shape),
            whole((1, width)),
            pl.BlockSpec((step, tokens), lambda i: (i, 0)),
        ],
        out_specs=(
            whole((tokens, width)),
            whole((tokens, width)),
            pl.BlockSpec((step, width), lambda i: (i, 0)),
        ),
        out_shape=(
            jax.ShapeDtypeStruct((tokens, width), BF16),
            jax.ShapeDtypeStruct((tokens, width), BF16),
            jax.ShapeDtypeStruct((rows, width), BF16),
        ),
        compiler_params=params(),
        name="norm_dispatch",
    )(parts, residual, gain.reshape(1, width), send)


def dispatch_kernel(send_ref, normed_ref, out_ref):
    out_ref[...] = jnp.dot(send_ref[...], normed_ref[...], preferred_element_type=F32).astype(BF16)


def dispatch(send, normed):
    tokens, width = normed.shape
    rows = send.shape[0]
    step = 256
    return pl.pallas_call(
        dispatch_kernel,
        grid=(rows // step,),
        in_specs=[
            pl.BlockSpec((step, tokens), lambda i: (i, 0)),
            pl.BlockSpec((tokens, width), lambda i: (0, 0)),
        ],
        out_specs=pl.BlockSpec((step, width), lambda i: (i, 0)),
        out_shape=jax.ShapeDtypeStruct((rows, width), BF16),
        compiler_params=params(),
        name="dispatch",
    )(send, normed)


def expert_kernel(x_ref, gate_up_ref, down_ref, out_ref):
    projected = jnp.dot(x_ref[...], gate_up_ref[0], preferred_element_type=F32)
    gate, up = projected[:, :FFE], projected[:, FFE:]
    hidden = (gate / (1.0 + jnp.exp(-gate)) * up).astype(BF16)
    out_ref[...] = jnp.dot(hidden, down_ref[0], preferred_element_type=F32).astype(BF16)


def expert(x, gate_up, down):
    rows, width = x.shape
    step = 256
    whole = lambda shape: pl.BlockSpec(
        shape, lambda i: (0,) * len(shape), pipeline_mode=pl.Buffered(1)
    )
    return pl.pallas_call(
        expert_kernel,
        grid=(rows // step,),
        in_specs=[
            pl.BlockSpec((step, width), lambda i: (i, 0)),
            whole(gate_up.shape),
            whole(down.shape),
        ],
        out_specs=pl.BlockSpec((step, width), lambda i: (i, 0)),
        out_shape=jax.ShapeDtypeStruct((rows, width), BF16),
        compiler_params=params(),
        name="expert",
    )(x, gate_up, down)


def combine_kernel(table_ref, rows_ref, *refs):
    before_ref, (out_ref, total_ref) = (refs[0] if len(refs) == 3 else None), refs[-2:]
    step = pl.program_id(0)
    tokens = out_ref.shape[0]
    part = lax.dot_general(table_ref[...], rows_ref[...], TN, preferred_element_type=F32)
    part = part[:tokens] + part[tokens:]

    @pl.when(step == 0)
    def _():
        total_ref[...] = part if before_ref is None else part + before_ref[...]

    @pl.when(step > 0)
    def _():
        total_ref[...] += part

    @pl.when(step == pl.num_programs(0) - 1)
    def _():
        out_ref[...] = total_ref[...].astype(out_ref.dtype)


def combine(table, rows, before, dtype):
    count, width = rows.shape
    tokens = table.shape[1] // 2
    step = 256
    whole = lambda shape: pl.BlockSpec(shape, lambda i: (0,) * len(shape))
    operands = (table, rows) + (() if before is None else (before,))
    return pl.pallas_call(
        combine_kernel,
        grid=(count // step,),
        in_specs=[
            pl.BlockSpec((step, 2 * tokens), lambda i: (i, 0)),
            pl.BlockSpec((step, width), lambda i: (i, 0)),
        ]
        + ([] if before is None else [whole(before.shape)]),
        out_specs=whole((tokens, width)),
        out_shape=jax.ShapeDtypeStruct((tokens, width), dtype),
        scratch_shapes=[pltpu.VMEM((tokens, width), F32)],
        compiler_params=params(),
        name="combine",
    )(*operands)


def body(
    queries,
    keys,
    values,
    distances,
    out_weight,
    residual,
    norm_gain,
    expert_gate_up,
    expert_down,
    routes,
    route_weights,
):
    length = queries.shape[0]
    tokens, width = residual.shape
    devices = lax.axis_size(ALL)
    group = lax.axis_size("head")
    source = lax.axis_index("ctx") - distances[0]
    usable = (source >= 0).astype(jnp.int32)
    packed = jnp.concatenate([keys, values], axis=1)
    everything = lax.all_gather(packed, "ctx", axis=0, tiled=True)
    offsets = jnp.maximum(source, 0) * length
    fetched = jnp.stack(
        [lax.dynamic_slice_in_dim(everything, offsets[j], length, 0) for j in range(DIST)]
    )
    far_keys, far_values = fetched[:, :, :HD], fetched[:, :, HD:]
    projected = attention(usable, queries, keys, values, far_keys, far_values, out_weight)
    parts = lax.all_to_all(projected, "head", split_axis=0, concat_axis=0, tiled=True)
    send, table = tables(routes, route_weights, devices)
    attended, normed, first = norm_dispatch(
        parts.reshape(group, tokens, width), residual, norm_gain, send[0]
    )
    exchange = lambda a: lax.all_to_all(a, ALL, split_axis=0, concat_axis=0, tiled=True)
    arrived = [exchange(first)]
    for c in range(1, CHUNKS):
        arrived.append(exchange(dispatch(send[c], normed)))
    returned = [exchange(expert(a, expert_gate_up, expert_down)) for a in arrived]
    total = None
    for c in range(CHUNKS):
        total = combine(table[c], returned[c], total, BF16 if c == CHUNKS - 1 else F32)
    return (attended, total)


def solution(mesh):
    return jax.shard_map(
        body,
        mesh=mesh,
        in_specs=(
            P("ctx", "head"),
            P("ctx", "head"),
            P("ctx", "head"),
            P("head", None),
            P("head", None),
            P(ALL, None),
            P(),
            P(ALL, None, None),
            P(ALL, None, None),
            P(ALL, None),
            P(ALL, None),
        ),
        out_specs=(P(ALL, None), P(ALL, None)),
        check_vma=False,
    )
```

time: 488 us -> 370 us (0.76); the launches traced: 478 us -> 369 us
  blocking collectives: 106 us -> 0 us
  Pallas kernels: 0 us -> 74.4 us
  local copies, waits for them, and re-layouts: 78.4 us -> 5.18 us
  matrix products: 65.5 us -> 0 us
  waiting for transfers between devices: 180 us -> 238 us
  starting transfers between devices: 5.32 us -> 25.5 us
  other arithmetic: 22.6 us -> 6.18 us
    all_to_all x1 -> x0, blocking collectives: 106 us -> none  [body(): lax.all_to_all(outgoing, ('ctx', 'head'), split_axis=0, concat_axis=0, ti...]
    all_to_all x1 -> x5, waiting for transfers between devices: 97.5 us -> 188 us  [the longest x4 168 us: body(): lax.all_to_all(a, ALL, split_axis=0, concat_axis=0, tiled=True)]
    pallas_call x0 -> x8, Pallas kernels: none -> 74.4 us  [the longest x2 31.1 us: expert(): pl.pallas_call(expert_kernel, grid=(rows // step,), in_specs=[pl.BlockSpe...]
    dot_general x7 -> x0, matrix products: 65.5 us -> none  [the longest x1 35.8 us: expert_rows(): jnp.einsum('sekd,edf->eskf', grid, expert_gate_up, preferred_element_type...]
    reduce_scatter x1 -> x0, waiting for transfers between devices: 42.7 us -> none  [body(): lax.psum_scatter(jnp.dot(attention, out_weight, preferred_element_type=jn...]
    unnamed x28 -> x6, local copies, waits for them, and re-layouts: 30.4 us -> 1.33 us
    gather x1 -> x0, local copies, waits for them, and re-layouts: 25.6 us -> none  [body(): picked = returned[flat_experts, places].astype(jnp.float32)]
    all_to_all x1 -> x5, starting transfers between devices: 5.24 us -> 25.4 us  [the longest x4 21.4 us: body(): lax.all_to_all(a, ALL, split_axis=0, concat_axis=0, tiled=True)]
  transfers between devices with their start and end apart: 3 -> 6, of which waited for: 3 -> 6; matrix products, arithmetic and copies ran while one was open for 3% -> 2% of each run, Pallas kernels for 0% -> 12%
where the time goes in v1:
time: 370 us; the launch traced here: 369 us
  waiting for transfers between devices  238 us (64%)
  Pallas kernels  74.4 us (20%)
  starting transfers between devices  25.5 us (7%)
  between operations  19.6 us (5%)
  other arithmetic  6.18 us (2%)
  local copies, waits for them, and re-layouts  5.18 us (1%)
    all_to_all x4, waiting for transfers between devices, body(): lax.all_to_all(a, ALL, split_axis=0, concat_axis=0, tiled=True)  168 us
    all_gather x1, waiting for transfers between devices, body(): everything = lax.all_gather(packed, 'ctx', axis=0, tiled=True)  50.6 us
    pallas_call x2, Pallas kernels, expert(): pl.pallas_call(expert_kernel, grid=(rows // step,), in_specs=[pl.BlockSpe...  31.1 us
    all_to_all x4, starting transfers between devices, body(): lax.all_to_all(a, ALL, split_axis=0, concat_axis=0, tiled=True)  21.4 us
    all_to_all x1, waiting for transfers between devices, body(): lax.all_to_all(projected, 'head', split_axis=0, concat_axis=0, tiled=True)  19.7 us
    pallas_call x1, Pallas kernels, attention(): pl.pallas_call(attention_kernel, grid_spec=pltpu.PrefetchScalarGridSpec(n...  17.4 us
    pallas_call x2, Pallas kernels, combine(): pl.pallas_call(combine_kernel, grid=(count // step,), in_specs=[pl.BlockS...  10.9 us
  transfers between devices with their start and end apart: 6, of which 6 were waited for; matrix products, arithmetic and copies ran while one was open for 2% of the time, Pallas kernels for 12%

profile of v1, /device:TPU:1, one launch (start us, length us, event | category | flops | bytes accessed | tf_op | source)
XLA Modules:
  0.0 369.2 jit_solution(3002277616695092897)
XLA Ops:
  7.2 0.0 all-gather.2.cloned.1.call-start
  7.2 1.7 pad_maximum_fusion.2
  8.9 0.7 maximum_multiply_fusion
  9.6 0.6 fusion.5
  15.7 1.2 fusion.3.usable
  16.9 50.6 %all-gather.2.cloned.1.call-done = bf16[16384,256]{1,0:T(8,128)(2,1)} async-done(((bf16[512,256]{1,0:T(8,128)(2,1)}), bf16[16384,256]{1,0:T(8,128)(2,1)}) %all-gather.2.cloned.1.call-update) | async-done | bytes 8388624 | tf_op jit(solution)/shard_map/all_gather | solution.py:286
  67.5 1.4 dynamic-slice_bitcast_fusion.2
  68.9 0.1 pad_maximum_fusion
  69.0 1.0 fusion.4
  70.0 17.4 %attention.1 = bf16[512,2048]{1,0:T(8,128)(2,1)} custom-call(s32[3]{0:T(128)} %fusion.3.usable, bf16[512,1024]{1,0:T(8,128)(2,1)} %q_ref.1, bf16[512,128]{1,0:T(8,128)(2,1)} %k_ref.1, bf16[512,128]{1,0:T(8,128)(2,1)} %v_ref.1, bf16[3,512,128]{2,1,0:T(8,128)(2,1)} %get-tuple-element.20.fk_ref, bf16[3,512,128]{2,1,0:T(8,128)(2,1)} %get-tuple-element.19.fv_ref, ...), custom_call_target="tpu_custom_call" | custom-call | tf_op jit(solution)/shard_map/attention/pallas_call | solution.py:70
  87.4 4.0 %all-to-all-start = ((bf16[4,128,2048]{2,1,0:T(8,128)(2,1)}), bf16[4,128,2048]{2,1,0:T(8,128)(2,1)S(1)}, u32[]{:S(2)}, u32[]{:S(2)}) async-start(bf16[4,128,2048]{2,1,0:T(8,128)(2,1)} %bitcast.38), calls=%async_computation | async-start | bytes 4194304 | tf_op jit(solution)/shard_map/all_to_all | solution.py:293
  91.4 4.1 %tables.1 = (f32[2,128,8,128]{3,2,1,0:T(8,128)}, f32[2,128,8,128]{3,2,1,0:T(8,128)}, f32[2,128,8,128]{3,2,1,0:T(8,128)}) custom-call(s32[8,128]{1,0:T(8,128)} %bitcast.41, f32[8,128]{1,0:T(8,128)} %bitcast.42), custom_call_target="tpu_custom_call" | custom-call | tf_op jit(solution)/shard_map/tables/pallas_call | solution.py:122
  95.5 1.3 convert_element_type.23
  96.8 0.9 slice_bitcast_fusion
  97.7 19.7 %all-to-all-done.parts_ref = bf16[4,128,2048]{2,1,0:T(8,128)(2,1)S(1)} async-done(((bf16[4,128,2048]{2,1,0:T(8,128)(2,1)}), bf16[4,128,2048]{2,1,0:T(8,128)(2,1)S(1)}, u32[]{:S(2)}, u32[]{:S(2)}) %all-to-all-start) | async-done | bytes 2097184 | tf_op jit(solution)/shard_map/all_to_all | solution.py:293
  117.4 1.3 copy-done
  118.7 6.0 %norm_dispatch.1 = (bf16[128,2048]{1,0:T(8,128)(2,1)}, bf16[128,2048]{1,0:T(8,128)(2,1)}, bf16[1024,2048]{1,0:T(8,128)(2,1)}) custom-call(bf16[4,128,2048]{2,1,0:T(8,128)(2,1)} %copy-done, bf16[128,2048]{1,0:T(8,128)(2,1)} %residual_ref.1, f32[1,2048]{1,0:T(1,128)} %bitcast.40, bf16[1024,128]{1,0:T(8,128)(2,1)} %get-tuple-element.22.send_ref), custom_call_target="tpu_custom_call" | custom-call | tf_op jit(solution)/shard_map/norm_dispatch/pallas_call | solution.py:150
  124.7 7.0 %all-to-all-start.3 = ((bf16[128,8,2048]{2,1,0:T(8,128)(2,1)}), bf16[128,8,2048]{2,1,0:T(8,128)(2,1)}, u32[]{:S(2)}, u32[]{:S(2)}) async-start(bf16[128,8,2048]{2,1,0:T(8,128)(2,1)} %bitcast.39), calls=%async_computation.3 | async-start | bytes 8388608 | tf_op jit(solution)/shard_map/all_to_all | solution.py:298
  131.8 4.8 %dispatch.1 = bf16[1024,2048]{1,0:T(8,128)(2,1)} custom-call(bf16[1024,128]{1,0:T(8,128)(2,1)} %get-tuple-element.21.send_ref, bf16[128,2048]{1,0:T(8,128)(2,1)} %get-tuple-element.12.normed_ref), custom_call_target="tpu_custom_call" | custom-call | tf_op jit(solution)/shard_map/dispatch/pallas_call | solution.py:182
  136.5 48.1 %all-to-all-done.3 = bf16[128,8,2048]{2,1,0:T(8,128)(2,1)} async-done(((bf16[128,8,2048]{2,1,0:T(8,128)(2,1)}), bf16[128,8,2048]{2,1,0:T(8,128)(2,1)}, u32[]{:S(2)}, u32[]{:S(2)}) %all-to-all-start.3) | async-done | bytes 4194336 | tf_op jit(solution)/shard_map/all_to_all | solution.py:298
  184.6 4.8 %all-to-all-start.1 = ((bf16[128,8,2048]{2,1,0:T(8,128)(2,1)}), bf16[128,8,2048]{2,1,0:T(8,128)(2,1)}, u32[]{:S(2)}, u32[]{:S(2)}) async-start(bf16[128,8,2048]{2,1,0:T(8,128)(2,1)} %bitcast.37), calls=%async_computation.1 | async-start | bytes 8388608 | tf_op jit(solution)/shard_map/all_to_all | solution.py:298
  189.4 15.5 %expert.3 = bf16[1024,2048]{1,0:T(8,128)(2,1)} custom-call(bf16[1024,2048]{1,0:T(8,128)(2,1)} %bitcast.22.x_ref, bf16[1,2048,1536]{2,1,0:T(8,128)(2,1)} %gate_up_ref.3, bf16[1,768,2048]{2,1,0:T(8,128)(2,1)} %down_ref.3), custom_call_target="tpu_custom_call" | custom-call | tf_op jit(solution)/shard_map/expert/pallas_call | solution.py:209
  204.9 37.1 %all-to-all-done.1 = bf16[128,8,2048]{2,1,0:T(8,128)(2,1)} async-done(((bf16[128,8,2048]{2,1,0:T(8,128)(2,1)}), bf16[128,8,2048]{2,1,0:T(8,128)(2,1)}, u32[]{:S(2)}, u32[]{:S(2)}) %all-to-all-start.1) | async-done | bytes 4194336 | tf_op jit(solution)/shard_map/all_to_all | solution.py:298
  242.0 4.8 %all-to-all-start.4 = ((bf16[128,8,2048]{2,1,0:T(8,128)(2,1)}), bf16[128,8,2048]{2,1,0:T(8,128)(2,1)}, u32[]{:S(2)}, u32[]{:S(2)}) async-start(bf16[128,8,2048]{2,1,0:T(8,128)(2,1)} %bitcast.36), calls=%async_computation.4 | async-start | bytes 8388608 | tf_op jit(solution)/shard_map/all_to_all | solution.py:298
  246.7 15.6 %expert.2 = bf16[1024,2048]{1,0:T(8,128)(2,1)} custom-call(bf16[1024,2048]{1,0:T(8,128)(2,1)} %bitcast.17.x_ref, bf16[1,2048,1536]{2,1,0:T(8,128)(2,1)} %gate_up_ref.3, bf16[1,768,2048]{2,1,0:T(8,128)(2,1)} %down_ref.3), custom_call_target="tpu_custom_call" | custom-call | tf_op jit(solution)/shard_map/expert/pallas_call | solution.py:209
  262.3 37.0 %all-to-all-done.4 = bf16[128,8,2048]{2,1,0:T(8,128)(2,1)} async-done(((bf16[128,8,2048]{2,1,0:T(8,128)(2,1)}), bf16[128,8,2048]{2,1,0:T(8,128)(2,1)}, u32[]{:S(2)}, u32[]{:S(2)}) %all-to-all-start.4) | async-done | bytes 4194336 | tf_op jit(solution)/shard_map/all_to_all | solution.py:298
  299.3 4.9 %all-to-all-start.2 = ((bf16[128,8,2048]{2,1,0:T(8,128)(2,1)}), bf16[128,8,2048]{2,1,0:T(8,128)(2,1)}, u32[]{:S(2)}, u32[]{:S(2)}) async-start(bf16[128,8,2048]{2,1,0:T(8,128)(2,1)} %bitcast.35), calls=%async_computation.2 | async-start | bytes 8388608 | tf_op jit(solution)/shard_map/all_to_all | solution.py:298
  304.2 0.1 convert_bitcast_fusion
  304.4 1.1 fusion.2
  305.5 5.4 %combine.2.refs_0_ = f32[128,2048]{1,0:T(8,128)} custom-call(bf16[1024,256]{1,0:T(8,128)(2,1)} %get-tuple-element.17.table_ref, bf16[1024,2048]{1,0:T(8,128)(2,1)} %bitcast.24.rows_ref), custom_call_target="tpu_custom_call" | custom-call | tf_op jit(solution)/shard_map/combine/pallas_call | solution.py:250
  310.9 45.9 %all-to-all-done.2 = bf16[128,8,2048]{2,1,0:T(8,128)(2,1)} async-done(((bf16[128,8,2048]{2,1,0:T(8,128)(2,1)}), bf16[128,8,2048]{2,1,0:T(8,128)(2,1)}, u32[]{:S(2)}, u32[]{:S(2)}) %all-to-all-start.2) | async-done | bytes 4194336 | tf_op jit(solution)/shard_map/all_to_all | solution.py:298
  356.8 5.5 %combine.3 = bf16[128,2048]{1,0:T(8,128)(2,1)} custom-call(bf16[1024,256]{1,0:T(8,128)(2,1)} %get-tuple-element.18.table_ref, bf16[1024,2048]{1,0:T(8,128)(2,1)} %bitcast.19.rows_ref, f32[128,2048]{1,0:T(8,128)} %combine.2.refs_0_), custom_call_target="tpu_custom_call" | custom-call | tf_op jit(solution)/shard_map/combine/pallas_call | solution.py:250
  (6 shorter events, 0.0 us)
Async XLA Ops:
  7.2 60.4 %all-gather.2.cloned.1.call-start = ((), (), s32[]{:S(2)}) async-start(), calls=%async_computation.5 | async-start | bytes 8650752 | tf_op jit(solution)/shard_map/all_gather | solution.py:286
  87.4 29.9 %all-to-all-start = ((bf16[4,128,2048]{2,1,0:T(8,128)(2,1)}), bf16[4,128,2048]{2,1,0:T(8,128)(2,1)S(1)}, u32[]{:S(2)}, u32[]{:S(2)}) async-start(bf16[4,128,2048]{2,1,0:T(8,128)(2,1)} %bitcast.38), calls=%async_computation | async-start | bytes 4194304 | tf_op jit(solution)/shard_map/all_to_all | solution.py:293
  117.4 1.3 copy-start
  124.7 59.9 %all-to-all-start.3 = ((bf16[128,8,2048]{2,1,0:T(8,128)(2,1)}), bf16[128,8,2048]{2,1,0:T(8,128)(2,1)}, u32[]{:S(2)}, u32[]{:S(2)}) async-start(bf16[128,8,2048]{2,1,0:T(8,128)(2,1)} %bitcast.39), calls=%async_computation.3 | async-start | bytes 8388608 | tf_op jit(solution)/shard_map/all_to_all | solution.py:298
  184.6 57.3 %all-to-all-start.1 = ((bf16[128,8,2048]{2,1,0:T(8,128)(2,1)}), bf16[128,8,2048]{2,1,0:T(8,128)(2,1)}, u32[]{:S(2)}, u32[]{:S(2)}) async-start(bf16[128,8,2048]{2,1,0:T(8,128)(2,1)} %bitcast.37), calls=%async_computation.1 | async-start | bytes 8388608 | tf_op jit(solution)/shard_map/all_to_all | solution.py:298
  242.0 57.3 %all-to-all-start.4 = ((bf16[128,8,2048]{2,1,0:T(8,128)(2,1)}), bf16[128,8,2048]{2,1,0:T(8,128)(2,1)}, u32[]{:S(2)}, u32[]{:S(2)}) async-start(bf16[128,8,2048]{2,1,0:T(8,128)(2,1)} %bitcast.36), calls=%async_computation.4 | async-start | bytes 8388608 | tf_op jit(solution)/shard_map/all_to_all | solution.py:298
  299.3 4.9 %copy-start.1 = (f32[2,128,8,128]{3,2,1,0:T(8,128)S(1)}, f32[2,128,8,128]{3,2,1,0:T(8,128)}, u32[]{:S(2)}) copy-start(f32[2,128,8,128]{3,2,1,0:T(8,128)} %get-tuple-element.10) | copy-start | bytes 3145732
  299.3 4.9 %copy-start.2 = (f32[2,128,8,128]{3,2,1,0:T(8,128)S(1)}, f32[2,128,8,128]{3,2,1,0:T(8,128)}, u32[]{:S(2)}) copy-start(f32[2,128,8,128]{3,2,1,0:T(8,128)} %get-tuple-element.11) | copy-start | bytes 3145732
  299.3 57.5 %all-to-all-start.2 = ((bf16[128,8,2048]{2,1,0:T(8,128)(2,1)}), bf16[128,8,2048]{2,1,0:T(8,128)(2,1)}, u32[]{:S(2)}, u32[]{:S(2)}) async-start(bf16[128,8,2048]{2,1,0:T(8,128)(2,1)} %bitcast.35), calls=%async_computation.2 | async-start | bytes 8388608 | tf_op jit(solution)/shard_map/all_to_all | solution.py:298
Sparse Core Ops, SparseCore 0:
  10.8 56.6 all-gather.1

commit v2 on v1

v2 whole, which is shorter than its diff:
```python
import functools
import math

import jax
import jax.numpy as jnp
from jax import lax
from jax.experimental import pallas as pl
from jax.experimental.pallas import tpu as pltpu
from jax.sharding import PartitionSpec as P

HD = 128
FFE = 768
TOP = 8
BLK = 128
DIST = 3
CAP = 16
CHUNKS = 2
ALL = ("ctx", "head")
BF16 = jnp.bfloat16
F32 = jnp.float32
NT = (((1,), (1,)), ((), ()))
TN = (((0,), (0,)), ((), ()))
EXPONENT = math.log2(math.e) / math.sqrt(HD)
VMEM_LIMIT = 56 * 1024 * 1024


def params(steps=1):
    return pltpu.CompilerParams(
        dimension_semantics=("arbitrary",) * steps, vmem_limit_bytes=VMEM_LIMIT
    )


def near_kernel(q_ref, k_ref, v_ref, mixed_ref, stats_ref):
    block = pl.program_id(0)
    heads = q_ref.shape[1] // HD
    blocks = k_ref.shape[0] // BLK

    def attend(at):
        near = at * BLK
        keys, values = k_ref[: near + BLK], v_ref[: near + BLK]
        rows = lax.broadcasted_iota(jnp.int32, (BLK, BLK), 0)
        columns = lax.broadcasted_iota(jnp.int32, (BLK, BLK), 1)
        bias = jnp.where(rows >= columns, 0.0, -jnp.inf)
        if at:
            bias = jnp.concatenate([jnp.zeros((BLK, near), F32), bias], axis=1)
        stats = jnp.zeros((BLK, HD), F32)
        for n in range(heads):
            query = q_ref[:, n * HD : (n + 1) * HD]
            score = lax.dot_general(query, keys, NT, preferred_element_type=F32) + bias
            highest = jnp.max(score, axis=1, keepdims=True)
            weight = jnp.exp2((score - highest) * EXPONENT)
            stats = jnp.where(columns == n, highest, stats)
            stats = jnp.where(
                columns == heads + n, jnp.sum(weight, axis=1, keepdims=True), stats
            )
            mixed_ref[:, n * HD : (n + 1) * HD] = jnp.dot(
                weight.astype(BF16), values, preferred_element_type=F32
            )
        stats_ref[...] = stats

    for at in range(blocks):
        pl.when(block == at)(functools.partial(attend, at))


def near_attention(queries, keys, values):
    length, wide = queries.shape
    whole = lambda shape: pl.BlockSpec(shape, lambda b: (0,) * len(shape))
    rows = lambda columns: pl.BlockSpec((BLK, columns), lambda b: (b, 0))
    return pl.pallas_call(
        near_kernel,
        grid=(length // BLK,),
        in_specs=[rows(wide), whole(keys.shape), whole(values.shape)],
        out_specs=(rows(wide), rows(HD)),
        out_shape=(
            jax.ShapeDtypeStruct((length, wide), F32),
            jax.ShapeDtypeStruct((length, HD), F32),
        ),
        compiler_params=params(),
        name="near_attention",
    )(queries, keys, values)


def far_kernel(
    place, wanted, q_ref, mine_ref, other_ref, near_ref, stats_ref, w_ref, out_ref, mixed_ref
):
    heads = q_ref.shape[1] // HD
    keys, values, bias = [], [], []
    for j in range(DIST):
        swapped = lax.rem(wanted[0, j], 2) > 0
        keys.append(jnp.where(swapped, other_ref[0, j], mine_ref[0, j]))
        values.append(jnp.where(swapped, other_ref[1, j], mine_ref[1, j]))
        reach = jnp.where(place[1] >= wanted[0, j], 0.0, -jnp.inf)
        bias.append(jnp.full((BLK, BLK), reach, F32))
    keys, values = jnp.concatenate(keys, axis=0), jnp.concatenate(values, axis=0)
    bias = jnp.concatenate(bias, axis=1)
    for n in range(heads):
        span = slice(n * HD, (n + 1) * HD)
        score = lax.dot_general(q_ref[:, span], keys, NT, preferred_element_type=F32) + bias
        before = stats_ref[:, n : n + 1]
        highest = jnp.maximum(jnp.max(score, axis=1, keepdims=True), before)
        weight = jnp.exp2((score - highest) * EXPONENT)
        keep = jnp.exp2((before - highest) * EXPONENT)
        denominator = jnp.sum(weight, axis=1, keepdims=True)
        denominator = denominator + keep * stats_ref[:, heads + n : heads + n + 1]
        mixed = jnp.dot(weight.astype(BF16), values, preferred_element_type=F32)
        mixed = mixed + keep * near_ref[:, span]
        mixed_ref[:, span] = (mixed / denominator).astype(BF16)
    out_ref[...] = jnp.dot(mixed_ref[...], w_ref[...], preferred_element_type=F32).astype(BF16)


def far_attention(place, wanted, queries, mine, other, near, stats, out_weight, count):
    wide, width = queries.shape[1], out_weight.shape[1]
    blocks = queries.shape[0] // BLK
    at = lambda i, place: lax.rem(place[0] + i, blocks)
    rows = lambda columns: pl.BlockSpec((BLK, columns), lambda i, p, w: (at(i, p), 0))
    far = pl.BlockSpec((2, DIST, BLK, HD), lambda i, p, w: (0, 0, at(i, p), 0))
    return pl.pallas_call(
        far_kernel,
        grid_spec=pltpu.PrefetchScalarGridSpec(
            num_scalar_prefetch=2,
            grid=(count,),
            in_specs=[
                rows(wide),
                far,
                far,
                rows(wide),
                rows(HD),
                pl.BlockSpec(
                    out_weight.shape, lambda i, p, w: (0, 0), pipeline_mode=pl.Buffered(1)
                ),
            ],
            out_specs=pl.BlockSpec((BLK, width), lambda i, p, w: (i, 0)),
            scratch_shapes=[pltpu.VMEM((BLK, wide), BF16)],
        ),
        out_shape=jax.ShapeDtypeStruct((count * BLK, width), BF16),
        compiler_params=params(),
        name="far_attention",
    )(place, wanted, queries, mine, other, near, stats, out_weight)


def pick_kernel(place, wanted, *refs):
    key_refs, value_refs, out_ref, sems = refs[:5], refs[5:10], refs[10], refs[11]
    me = place[0]
    core = lax.rem(me, 2)
    for j in range(DIST):
        asked = me - core + lax.rem(core + wanted[0, j], 2)
        source = asked - wanted[0, j]
        source = jnp.where(source >= 0, source, me)
        over_z = lax.rem(me // 8 - source // 8 + 4, 4)
        over_x = lax.rem(lax.rem(me // 2, 4) - lax.rem(source // 2, 4) + 4, 4)
        for kind, pieces, outer, inner in (
            (0, key_refs, over_x, over_z),
            (1, value_refs, over_z, over_x),
        ):
            target, sem = out_ref.at[kind, j], sems.at[kind, j]

            def fetch(piece, row, target=target, sem=sem):
                pltpu.make_async_copy(piece.at[row], target, sem).start()

            for step in (0, 1, 3):
                pl.when(outer == step)(functools.partial(fetch, pieces[step], inner))
            pl.when((outer == 2) & (inner < 2))(functools.partial(fetch, pieces[2], inner))
            pl.when((outer == 2) & (inner >= 2))(functools.partial(fetch, pieces[4], inner - 2))
    for j in range(DIST):
        for kind, pieces in ((0, key_refs), (1, value_refs)):
            pltpu.make_async_copy(
                pieces[0].at[0], out_ref.at[kind, j], sems.at[kind, j]
            ).wait()


def pick(place, wanted, key_pieces, value_pieces):
    anywhere = pl.BlockSpec(memory_space=pl.ANY)
    length = key_pieces[0].shape[1]
    return pl.pallas_call(
        pick_kernel,
        grid_spec=pltpu.PrefetchScalarGridSpec(
            num_scalar_prefetch=2,
            grid=(1,),
            in_specs=[anywhere] * 10,
            out_specs=anywhere,
            scratch_shapes=[pltpu.SemaphoreType.DMA((2, DIST))],
        ),
        out_shape=jax.ShapeDtypeStruct((2, DIST, length, HD), BF16),
        compiler_params=params(),
        name="pick",
    )(place, wanted, *key_pieces, *value_pieces)


def moves(side):
    def along_z(step):
        return [(i, (i + 8 * step) % 32) for i in range(32)]

    def along_x(step):
        return [(i, i - i % 8 + (i + 2 * step) % 8) for i in range(32)]

    return (along_z if side == "z" else along_x)(1), (along_z if side == "z" else along_x)(-1)


def circle(block, side, axis):
    forward, backward = moves(side)
    send = lambda a, pairs: lax.ppermute(a, "ctx", pairs)
    half = block.shape[axis] // 2
    low = lambda a: lax.slice_in_dim(a, 0, half, axis=axis)
    high = lambda a: lax.slice_in_dim(a, half, 2 * half, axis=axis)
    one, three = send(block, forward), send(block, backward)
    return one, send(low(one), forward), three, send(high(three), backward)


def tables_kernel(routes_ref, weights_ref, send_ref, table_ref, spread_ref):
    top, tokens = routes_ref.shape
    experts, slots = spread_ref.shape[:2]
    chunks = send_ref.shape[0]
    names = lax.broadcasted_iota(jnp.int32, (experts, tokens), 0)
    chosen = jnp.zeros((experts, tokens), F32)
    weight = jnp.zeros((experts, tokens), F32)
    for k in range(top):
        here = routes_ref[k : k + 1, :] == names
        chosen = jnp.where(here, 1.0, chosen)
        weight = jnp.where(here, weights_ref[k : k + 1, :], weight)
    before = (
        lax.broadcasted_iota(jnp.int32, (tokens, tokens), 0)
        < lax.broadcasted_iota(jnp.int32, (tokens, tokens), 1)
    ).astype(BF16)
    place = jnp.dot(chosen.astype(BF16), before, preferred_element_type=F32)
    place = jnp.where(chosen > 0.0, place, -1.0)
    high = weight.astype(BF16).astype(F32)
    low = weight - high

    def spread(c, value):
        for s in range(slots):
            spread_ref[:, s, :] = jnp.where(place == float(c * slots + s), value, 0.0)
        return spread_ref[...].reshape(experts * slots, tokens).astype(BF16)

    for c in range(chunks):
        send_ref[c] = spread(c, 1.0)
        table_ref[c, :, :tokens] = spread(c, high)
        table_ref[c, :, tokens:] = spread(c, low)


def tables(routes, route_weights, experts):
    tokens = routes.shape[0]
    slots = CAP // CHUNKS
    return pl.pallas_call(
        tables_kernel,
        out_shape=(
            jax.ShapeDtypeStruct((CHUNKS, experts * slots, tokens), BF16),
            jax.ShapeDtypeStruct((CHUNKS, experts * slots, 2 * tokens), BF16),
        ),
        scratch_shapes=[pltpu.VMEM((experts, slots, tokens), F32)],
        compiler_params=params(0),
        name="tables",
    )(routes.T, route_weights.T)


def norm_kernel(
    own_ref, left_ref, right_ref, residual_ref, gain_ref, send_ref, attended_ref, normed_ref, out_ref
):
    @pl.when(pl.program_id(0) == 0)
    def _():
        total = residual_ref[...].astype(F32) + own_ref[...].astype(F32)
        total = total + left_ref[...].astype(F32) + right_ref[...].astype(F32)
        attended = total.astype(BF16)
        attended_ref[...] = attended
        wide = attended.astype(F32)
        inverse = lax.rsqrt(jnp.mean(wide * wide, axis=1, keepdims=True) + 1e-06)
        normed_ref[...] = (wide * inverse * gain_ref[...]).astype(BF16)

    out_ref[...] = jnp.dot(send_ref[0], normed_ref[...], preferred_element_type=F32).astype(BF16)


def norm_dispatch(own, left, right, residual, gain, send):
    tokens, width = residual.shape
    rows = send.shape[1]
    step = 256
    whole = lambda shape: pl.BlockSpec(shape, lambda i: (0,) * len(shape))
    return pl.pallas_call(
        norm_kernel,
        grid=(rows // step,),
        in_specs=[whole((tokens, width))] * 4
        + [whole((1, width)), pl.BlockSpec((1, step, tokens), lambda i: (0, i, 0))],
        out_specs=(
            whole((tokens, width)),
            whole((tokens, width)),
            pl.BlockSpec((step, width), lambda i: (i, 0)),
        ),
        out_shape=(
            jax.ShapeDtypeStruct((tokens, width), BF16),
            jax.ShapeDtypeStruct((tokens, width), BF16),
            jax.ShapeDtypeStruct((rows, width), BF16),
        ),
        compiler_params=params(),
        name="norm_dispatch",
    )(own, left, right, residual, gain.reshape(1, width), send)


def dispatch_kernel(send_ref, normed_ref, out_ref):
    out_ref[...] = jnp.dot(send_ref[0], normed_ref[...], preferred_element_type=F32).astype(BF16)


def dispatch(send, normed, chunk):
    tokens, width = normed.shape
    rows = send.shape[1]
    step = 256
    return pl.pallas_call(
        dispatch_kernel,
        grid=(rows // step,),
        in_specs=[
            pl.BlockSpec((1, step, tokens), lambda i: (chunk, i, 0)),
            pl.BlockSpec((tokens, width), lambda i: (0, 0)),
        ],
        out_specs=pl.BlockSpec((step, width), lambda i: (i, 0)),
        out_shape=jax.ShapeDtypeStruct((rows, width), BF16),
        compiler_params=params(),
        name="dispatch",
    )(send, normed)


def expert_kernel(x_ref, gate_up_ref, down_ref, out_ref):
    projected = jnp.dot(x_ref[...], gate_up_ref[0], preferred_element_type=F32)
    gate, up = projected[:, :FFE], projected[:, FFE:]
    hidden = (gate / (1.0 + jnp.exp(-gate)) * up).astype(BF16)
    out_ref[...] = jnp.dot(hidden, down_ref[0], preferred_element_type=F32).astype(BF16)


def expert(x, gate_up, down):
    rows, width = x.shape
    step = 256
    whole = lambda shape: pl.BlockSpec(
        shape, lambda i: (0,) * len(shape), pipeline_mode=pl.Buffered(1)
    )
    return pl.pallas_call(
        expert_kernel,
        grid=(rows // step,),
        in_specs=[
            pl.BlockSpec((step, width), lambda i: (i, 0)),
            whole(gate_up.shape),
            whole(down.shape),
        ],
        out_specs=pl.BlockSpec((step, width), lambda i: (i, 0)),
        out_shape=jax.ShapeDtypeStruct((rows, width), BF16),
        compiler_params=params(),
        name="expert",
    )(x, gate_up, down)


def combine_kernel(table_ref, rows_ref, *refs):
    before_ref, (out_ref, total_ref) = (refs[0] if len(refs) == 3 else None), refs[-2:]
    step = pl.program_id(0)
    tokens = out_ref.shape[0]
    part = lax.dot_general(table_ref[0], rows_ref[...], TN, preferred_element_type=F32)
    part = part[:tokens] + part[tokens:]

    @pl.when(step == 0)
    def _():
        total_ref[...] = part if before_ref is None else part + before_ref[...]

    @pl.when(step > 0)
    def _():
        total_ref[...] += part

    @pl.when(step == pl.num_programs(0) - 1)
    def _():
        out_ref[...] = total_ref[...].astype(out_ref.dtype)


def combine(table, rows, before, dtype, chunk):
    count, width = rows.shape
    tokens = table.shape[2] // 2
    step = 256
    whole = lambda shape: pl.BlockSpec(shape, lambda i: (0,) * len(shape))
    operands = (table, rows) + (() if before is None else (before,))
    return pl.pallas_call(
        combine_kernel,
        grid=(count // step,),
        in_specs=[
            pl.BlockSpec((1, step, 2 * tokens), lambda i: (chunk, i, 0)),
            pl.BlockSpec((step, width), lambda i: (i, 0)),
        ]
        + ([] if before is None else [whole(before.shape)]),
        out_specs=whole((tokens, width)),
        out_shape=jax.ShapeDtypeStruct((tokens, width), dtype),
        scratch_shapes=[pltpu.VMEM((tokens, width), F32)],
        compiler_params=params(),
        name="combine",
    )(*operands)


def body(
    queries,
    keys,
    values,
    distances,
    out_weight,
    residual,
    norm_gain,
    expert_gate_up,
    expert_down,
    routes,
    route_weights,
):
    tokens, width = residual.shape
    devices = lax.axis_size(ALL)
    me, head = lax.axis_index("ctx"), lax.axis_index("head")
    k1, k2a, k3, k2b = circle(keys, "z", 0)
    v1, v2a, v3, v2b = circle(values, "x", 0)
    key_line = jnp.stack([keys, k1, jnp.concatenate([k2a, k2b], axis=0), k3])
    value_line = jnp.stack([values, v1, jnp.concatenate([v2a, v2b], axis=0), v3])
    key_pieces = (key_line,) + circle(key_line, "x", 0)
    value_pieces = (value_line,) + circle(value_line, "z", 0)
    near, stats = near_attention(queries, keys, values)
    send, table = tables(routes, route_weights, devices)
    mine = pick(me.reshape(1), distances, key_pieces, value_pieces)
    other = lax.ppermute(mine, "ctx", [(i, i ^ 1) for i in range(32)])

    def project(first, count):
        place = jnp.stack([lax.rem(head + first, 4), me])
        return far_attention(
            place, distances, queries, mine, other, near, stats, out_weight, count
        )

    up = [(i, (i + 1) % 4) for i in range(4)]
    down = [(i, (i + 3) % 4) for i in range(4)]
    over_head = lambda a, pairs: lax.ppermute(a, "head", pairs)
    half = width // 2
    across = project(2, 1)
    from_left = over_head(across[:, :half], up)
    from_right = over_head(across[:, half:], down)
    after = project(1, 1)
    before = project(3, 1)
    add = lambda a, b: (a.astype(F32) + b.astype(F32)).astype(BF16)
    after = jnp.concatenate([add(after[:, :half], from_left), after[:, half:]], axis=1)
    before = jnp.concatenate([before[:, :half], add(before[:, half:], from_right)], axis=1)
    left, right = over_head(after, up), over_head(before, down)
    own = project(0, 1)
    attended, normed, first = norm_dispatch(own, left, right, residual, norm_gain, send)
    exchange = lambda a: lax.all_to_all(a, ALL, split_axis=0, concat_axis=0, tiled=True)
    arrived = [exchange(first)]
    for c in range(1, CHUNKS):
        arrived.append(exchange(dispatch(send, normed, c)))
    returned = [exchange(expert(a, expert_gate_up, expert_down)) for a in arrived]
    total = None
    for c in range(CHUNKS):
        total = combine(table, returned[c], total, BF16 if c == CHUNKS - 1 else F32, c)
    return (attended, total)


def solution(mesh):
    return jax.shard_map(
        body,
        mesh=mesh,
        in_specs=(
            P("ctx", "head"),
            P("ctx", "head"),
            P("ctx", "head"),
            P("head", None),
            P("head", None),
            P(ALL, None),
            P(),
            P(ALL, None, None),
            P(ALL, None, None),
            P(ALL, None),
            P(ALL, None),
        ),
        out_specs=(P(ALL, None), P(ALL, None)),
        check_vma=False,
    )
```

time: 370 us -> 381 us (1.030)
  waiting for transfers between devices: 238 us -> 187 us
  Pallas kernels: 74.4 us -> 125 us
  starting transfers between devices: 25.5 us -> 55.3 us
  between operations: 19.6 us -> 0.86 us
    all_gather x1 -> x0, waiting for transfers between devices: 50.6 us -> none  [body(): everything = lax.all_gather(packed, 'ctx', axis=0, tiled=True)]
    pallas_call x3 -> x8, Pallas kernels: 27.6 us -> 78 us  [the longest x4 33 us: far_attention(): pl.pallas_call(far_kernel, grid_spec=pltpu.PrefetchScalarGridSpec(num_sca...]
    ppermute x0 -> x21, starting transfers between devices: none -> 34.1 us  [the longest x16 22.3 us: circle(): send = lambda a, pairs: lax.ppermute(a, 'ctx', pairs)]
    all_to_all x1 -> x0, waiting for transfers between devices: 19.7 us -> none  [body(): lax.all_to_all(projected, 'head', split_axis=0, concat_axis=0, tiled=True)]
    ppermute x0 -> x21, waiting for transfers between devices: none -> 18 us  [the longest x16 13 us: circle(): send = lambda a, pairs: lax.ppermute(a, 'ctx', pairs)]
    another operation x1 -> x8, other arithmetic: 0.09 us -> 4.39 us  [the longest x4 2.42 us: project(): place = jnp.stack([lax.rem(head + first, 4), me])]
    all_to_all x1 -> x0, starting transfers between devices: 4 us -> none  [body(): lax.all_to_all(projected, 'head', split_axis=0, concat_axis=0, tiled=True)]
  transfers between devices with their start and end apart: 6 -> 25, of which waited for: 6 -> 8; matrix products, arithmetic and copies ran while one was open for 2% -> 2% of each run, Pallas kernels for 12% -> 21%
where the time goes in v2:
time: 381 us; the launch traced here: 380 us
  waiting for transfers between devices  187 us (49%)
  Pallas kernels  125 us (33%)
  starting transfers between devices  55.3 us (15%)
  local copies, waits for them, and re-layouts  6.27 us (2%)
  other arithmetic  5.54 us (1%)
    all_to_all x4, waiting for transfers between devices, body(): lax.all_to_all(a, ALL, split_axis=0, concat_axis=0, tiled=True)  169 us
    pallas_call x4, Pallas kernels, far_attention(): pl.pallas_call(far_kernel, grid_spec=pltpu.PrefetchScalarGridSpec(num_sca...  33 us
    pallas_call x2, Pallas kernels, expert(): pl.pallas_call(expert_kernel, grid=(rows // step,), in_specs=[pl.BlockSpe...  31.1 us
    pallas_call x1, Pallas kernels, pick(): pl.pallas_call(pick_kernel, grid_spec=pltpu.PrefetchScalarGridSpec(num_sc...  25.7 us
    ppermute x16, starting transfers between devices, circle(): send = lambda a, pairs: lax.ppermute(a, 'ctx', pairs)  22.3 us
    all_to_all x4, starting transfers between devices, body(): lax.all_to_all(a, ALL, split_axis=0, concat_axis=0, tiled=True)  21.3 us
    ppermute x16, waiting for transfers between devices, circle(): send = lambda a, pairs: lax.ppermute(a, 'ctx', pairs)  13 us
    pallas_call x2, Pallas kernels, combine(): pl.pallas_call(combine_kernel, grid=(count // step,), in_specs=[pl.BlockS...  10.9 us
  transfers between devices with their start and end apart: 25, of which 8 were waited for; matrix products, arithmetic and copies ran while one was open for 2% of the time, Pallas kernels for 21%

profile of v2, /device:TPU:1, one launch (start us, length us, event | category | flops | bytes accessed | tf_op | source)
XLA Modules:
  0.0 380.2 jit_solution(7398703447062608143)
XLA Ops:
  5.8 2.1 collective-permute-start.2
  8.1 2.7 collective-permute-start.11
  11.8 2.2 collective-permute-start.3
  17.6 2.7 collective-permute-start.6
  20.3 6.5 %collective-permute-done.14.refs_8_ = bf16[4,512,128]{2,1,0:T(8,128)(2,1)S(1)} collective-permute-done((bf16[4,512,128]{2,1,0:T(8,128)(2,1)S(1)}, bf16[4,512,128]{2,1,0:T(8,128)(2,1)S(1)}, u32[]{:S(2)}, u32[]{:S(2)}) %collective-permute-start.14) | collective-permute-done | bytes 524320 | tf_op jit(solution)/shard_map/ppermute | solution.py:201
  26.8 3.2 collective-permute-start.15
  33.8 3.7 collective-permute-done.13.refs_7_
  37.5 2.8 collective-permute-done.5.refs_2_
  40.4 25.7 %pick.1.mine_ref = bf16[2,3,512,128]{3,2,1,0:T(8,128)(2,1)} custom-call(s32[1]{0:T(128)} %bitcast.1.place, s32[1,3]{1,0:T(1,128)} %wanted.9, bf16[4,512,128]{2,1,0:T(8,128)(2,1)} %copy-done.3, bf16[4,512,128]{2,1,0:T(8,128)(2,1)} %copy-done.7, bf16[2,512,128]{2,1,0:T(8,128)(2,1)} %collective-permute-done.5.refs_2_, bf16[4,512,128]{2,1,0:T(8,128)(2,1)} %copy-done.6, ...), custom_call_target="tpu_custom_call" | custom-call | tf_op jit(solution)/shard_map/pick/pallas_call | solution.py:174
  66.1 5.6 %collective-permute-start.16 = (bf16[2,3,512,128]{3,2,1,0:T(8,128)(2,1)}, bf16[2,3,512,128]{3,2,1,0:T(8,128)(2,1)S(1)}, u32[]{:S(2)}, u32[]{:S(2)}) collective-permute-start(bf16[2,3,512,128]{3,2,1,0:T(8,128)(2,1)} %pick.1.mine_ref), channel_id=1, source_target_pairs={{0,4},{4,0},{8,12},{12,8},{16,20},{20,16},{24,28},{28,24},{32,36},... | collective-permute-start | bytes 2359304 | tf_op jit(solution)/shard_map/ppermute | solution.py:413
  71.7 9.6 %near_attention.1 = (f32[512,1024]{1,0:T(8,128)}, f32[512,128]{1,0:T(8,128)}) custom-call(bf16[512,1024]{1,0:T(8,128)(2,1)} %q_ref.9, bf16[512,128]{1,0:T(8,128)(2,1)} %k_ref.1, bf16[512,128]{1,0:T(8,128)(2,1)} %v_ref.1), custom_call_target="tpu_custom_call" | custom-call | tf_op jit(solution)/shard_map/near_attention/pallas_call | solution.py:69
  82.7 8.2 %far_attention.6 = bf16[128,2048]{1,0:T(8,128)(2,1)} custom-call(s32[2]{0:T(128)} %pad_add_fusion.2.place, s32[1,3]{1,0:T(1,128)} %wanted.9, bf16[512,1024]{1,0:T(8,128)(2,1)} %q_ref.9, bf16[2,3,512,128]{3,2,1,0:T(8,128)(2,1)} %pick.1.mine_ref, bf16[2,3,512,128]{3,2,1,0:T(8,128)(2,1)} %copy-done, f32[512,1024]{1,0:T(8,128)} %get-tuple-element.9.near_ref, ...), custom_call_target="tpu_custom_call" | custom-call | tf_op jit(solution)/shard_map/far_attention/pallas_call | solution.py:117
  94.9 8.2 %far_attention.7 = bf16[128,2048]{1,0:T(8,128)(2,1)} custom-call(s32[2]{0:T(128)} %pad_add_fusion.3.place, s32[1,3]{1,0:T(1,128)} %wanted.9, bf16[512,1024]{1,0:T(8,128)(2,1)} %q_ref.9, bf16[2,3,512,128]{3,2,1,0:T(8,128)(2,1)} %pick.1.mine_ref, bf16[2,3,512,128]{3,2,1,0:T(8,128)(2,1)} %copy-done, f32[512,1024]{1,0:T(8,128)} %get-tuple-element.9.near_ref, ...), custom_call_target="tpu_custom_call" | custom-call | tf_op jit(solution)/shard_map/far_attention/pallas_call | solution.py:117
  103.1 8.4 %far_attention.5 = bf16[128,2048]{1,0:T(8,128)(2,1)} custom-call(s32[2]{0:T(128)} %pad_add_fusion.1.place, s32[1,3]{1,0:T(1,128)} %wanted.9, bf16[512,1024]{1,0:T(8,128)(2,1)} %q_ref.9, bf16[2,3,512,128]{3,2,1,0:T(8,128)(2,1)} %pick.1.mine_ref, bf16[2,3,512,128]{3,2,1,0:T(8,128)(2,1)} %copy-done, f32[512,1024]{1,0:T(8,128)} %get-tuple-element.9.near_ref, ...), custom_call_target="tpu_custom_call" | custom-call | tf_op jit(solution)/shard_map/far_attention/pallas_call | solution.py:117
  115.1 5.0 %collective-permute-done.19 = bf16[128,1024]{1,0:T(8,128)(2,1)S(1)} collective-permute-done((bf16[128,1024]{1,0:T(8,128)(2,1)S(1)}, bf16[128,1024]{1,0:T(8,128)(2,1)S(1)}, u32[]{:S(2)}, u32[]{:S(2)}) %collective-permute-start.19) | collective-permute-done | bytes 262176 | tf_op jit(solution)/shard_map/ppermute | solution.py:423
  120.2 3.0 collective-permute-start.20
  123.2 3.9 %tables.1 = (bf16[2,1024,128]{2,1,0:T(8,128)(2,1)}, bf16[2,1024,256]{2,1,0:T(8,128)(2,1)}) custom-call(s32[8,128]{1,0:T(8,128)} %bitcast.37, f32[8,128]{1,0:T(8,128)} %bitcast.38), custom_call_target="tpu_custom_call" | custom-call | tf_op jit(solution)/shard_map/tables/pallas_call | solution.py:243
  127.8 8.2 %far_attention.4.own_ref = bf16[128,2048]{1,0:T(8,128)(2,1)} custom-call(s32[2]{0:T(128)} %pad_add_fusion.place, s32[1,3]{1,0:T(1,128)} %wanted.9, bf16[512,1024]{1,0:T(8,128)(2,1)} %q_ref.9, bf16[2,3,512,128]{3,2,1,0:T(8,128)(2,1)} %pick.1.mine_ref, bf16[2,3,512,128]{3,2,1,0:T(8,128)(2,1)} %copy-done, f32[512,1024]{1,0:T(8,128)} %get-tuple-element.9.near_ref, ...), custom_call_target="tpu_custom_call" | custom-call | tf_op jit(solution)/shard_map/far_attention/pallas_call | solution.py:117
  137.0 5.7 %norm_dispatch.1 = (bf16[128,2048]{1,0:T(8,128)(2,1)}, bf16[128,2048]{1,0:T(8,128)(2,1)}, bf16[1024,2048]{1,0:T(8,128)(2,1)}) custom-call(bf16[128,2048]{1,0:T(8,128)(2,1)} %far_attention.4.own_ref, bf16[128,2048]{1,0:T(8,128)(2,1)} %copy-done.8, bf16[128,2048]{1,0:T(8,128)(2,1)} %copy-done.9, bf16[128,2048]{1,0:T(8,128)(2,1)} %residual_ref.1, ...), custom_call_target="tpu_custom_call" | custom-call | tf_op jit(solution)/shard_map/norm_dispatch/pallas_call | solution.py:276
  142.7 7.0 %all-to-all-start.2 = ((bf16[128,8,2048]{2,1,0:T(8,128)(2,1)}), bf16[128,8,2048]{2,1,0:T(8,128)(2,1)}, u32[]{:S(2)}, u32[]{:S(2)}) async-start(bf16[128,8,2048]{2,1,0:T(8,128)(2,1)} %bitcast.29), calls=%async_computation.2 | async-start | bytes 8388608 | tf_op jit(solution)/shard_map/all_to_all | solution.py:436
  149.7 4.8 %dispatch.1 = bf16[1024,2048]{1,0:T(8,128)(2,1)} custom-call(bf16[2,1024,128]{2,1,0:T(8,128)(2,1)} %get-tuple-element.11.send_ref, bf16[128,2048]{1,0:T(8,128)(2,1)} %get-tuple-element.14.normed_ref), custom_call_target="tpu_custom_call" | custom-call | tf_op jit(solution)/shard_map/dispatch/pallas_call | solution.py:304
  154.5 48.1 %all-to-all-done.2 = bf16[128,8,2048]{2,1,0:T(8,128)(2,1)} async-done(((bf16[128,8,2048]{2,1,0:T(8,128)(2,1)}), bf16[128,8,2048]{2,1,0:T(8,128)(2,1)}, u32[]{:S(2)}, u32[]{:S(2)}) %all-to-all-start.2) | async-done | bytes 4194336 | tf_op jit(solution)/shard_map/all_to_all | solution.py:436
  202.5 4.8 %all-to-all-start = ((bf16[128,8,2048]{2,1,0:T(8,128)(2,1)}), bf16[128,8,2048]{2,1,0:T(8,128)(2,1)}, u32[]{:S(2)}, u32[]{:S(2)}) async-start(bf16[128,8,2048]{2,1,0:T(8,128)(2,1)} %bitcast.28), calls=%async_computation | async-start | bytes 8388608 | tf_op jit(solution)/shard_map/all_to_all | solution.py:436
  207.3 15.5 %expert.3 = bf16[1024,2048]{1,0:T(8,128)(2,1)} custom-call(bf16[1024,2048]{1,0:T(8,128)(2,1)} %bitcast.21.x_ref, bf16[1,2048,1536]{2,1,0:T(8,128)(2,1)} %gate_up_ref.3, bf16[1,768,2048]{2,1,0:T(8,128)(2,1)} %down_ref.3), custom_call_target="tpu_custom_call" | custom-call | tf_op jit(solution)/shard_map/expert/pallas_call | solution.py:331
  222.8 37.1 %all-to-all-done = bf16[128,8,2048]{2,1,0:T(8,128)(2,1)} async-done(((bf16[128,8,2048]{2,1,0:T(8,128)(2,1)}), bf16[128,8,2048]{2,1,0:T(8,128)(2,1)}, u32[]{:S(2)}, u32[]{:S(2)}) %all-to-all-start) | async-done | bytes 4194336 | tf_op jit(solution)/shard_map/all_to_all | solution.py:436
  259.9 4.8 %all-to-all-start.3 = ((bf16[128,8,2048]{2,1,0:T(8,128)(2,1)}), bf16[128,8,2048]{2,1,0:T(8,128)(2,1)}, u32[]{:S(2)}, u32[]{:S(2)}) async-start(bf16[128,8,2048]{2,1,0:T(8,128)(2,1)} %bitcast.27), calls=%async_computation.3 | async-start | bytes 8388608 | tf_op jit(solution)/shard_map/all_to_all | solution.py:436
  264.7 15.6 %expert.2 = bf16[1024,2048]{1,0:T(8,128)(2,1)} custom-call(bf16[1024,2048]{1,0:T(8,128)(2,1)} %bitcast.17.x_ref, bf16[1,2048,1536]{2,1,0:T(8,128)(2,1)} %gate_up_ref.3, bf16[1,768,2048]{2,1,0:T(8,128)(2,1)} %down_ref.3), custom_call_target="tpu_custom_call" | custom-call | tf_op jit(solution)/shard_map/expert/pallas_call | solution.py:331
  280.2 37.0 %all-to-all-done.3 = bf16[128,8,2048]{2,1,0:T(8,128)(2,1)} async-done(((bf16[128,8,2048]{2,1,0:T(8,128)(2,1)}), bf16[128,8,2048]{2,1,0:T(8,128)(2,1)}, u32[]{:S(2)}, u32[]{:S(2)}) %all-to-all-start.3) | async-done | bytes 4194336 | tf_op jit(solution)/shard_map/all_to_all | solution.py:436
  317.3 4.8 %all-to-all-start.1 = ((bf16[128,8,2048]{2,1,0:T(8,128)(2,1)}), bf16[128,8,2048]{2,1,0:T(8,128)(2,1)}, u32[]{:S(2)}, u32[]{:S(2)}) async-start(bf16[128,8,2048]{2,1,0:T(8,128)(2,1)} %bitcast.26), calls=%async_computation.1 | async-start | bytes 8388608 | tf_op jit(solution)/shard_map/all_to_all | solution.py:436
  322.0 5.4 %combine.2.refs_0_ = f32[128,2048]{1,0:T(8,128)} custom-call(bf16[2,1024,256]{2,1,0:T(8,128)(2,1)} %get-tuple-element.13.table_ref, bf16[1024,2048]{1,0:T(8,128)(2,1)} %bitcast.23.rows_ref), custom_call_target="tpu_custom_call" | custom-call | tf_op jit(solution)/shard_map/combine/pallas_call | solution.py:372
  327.4 47.2 %all-to-all-done.1 = bf16[128,8,2048]{2,1,0:T(8,128)(2,1)} async-done(((bf16[128,8,2048]{2,1,0:T(8,128)(2,1)}), bf16[128,8,2048]{2,1,0:T(8,128)(2,1)}, u32[]{:S(2)}, u32[]{:S(2)}) %all-to-all-start.1) | async-done | bytes 4194336 | tf_op jit(solution)/shard_map/all_to_all | solution.py:436
  374.6 5.5 %combine.3 = bf16[128,2048]{1,0:T(8,128)(2,1)} custom-call(bf16[2,1024,256]{2,1,0:T(8,128)(2,1)} %get-tuple-element.13.table_ref, bf16[1024,2048]{1,0:T(8,128)(2,1)} %bitcast.19.rows_ref, f32[128,2048]{1,0:T(8,128)} %combine.2.refs_0_), custom_call_target="tpu_custom_call" | custom-call | tf_op jit(solution)/shard_map/combine/pallas_call | solution.py:372
  (75 shorter events, 24.3 us)
Async XLA Ops:
  0.6 7.3 %collective-permute-start.8 = (bf16[512,128]{1,0:T(8,128)(2,1)}, bf16[512,128]{1,0:T(8,128)(2,1)S(1)}, u32[]{:S(2)}, u32[]{:S(2)}) collective-permute-start(bf16[512,128]{1,0:T(8,128)(2,1)} %v_ref.1), channel_id=1, source_target_pairs={{0,8},{4,12},{8,16},{12,20},{16,24},{20,28},{24,0},{28,4},{32,40},... | collective-permute-start | bytes 393224 | tf_op jit(solution)/shard_map/ppermute | solution.py:201
  2.7 5.3 %collective-permute-start.10 = (bf16[512,128]{1,0:T(8,128)(2,1)}, bf16[512,128]{1,0:T(8,128)(2,1)S(1)}, u32[]{:S(2)}, u32[]{:S(2)}) collective-permute-start(bf16[512,128]{1,0:T(8,128)(2,1)} %v_ref.1), channel_id=1, source_target_pairs={{0,24},{4,28},{8,0},{12,4},{16,8},{20,12},{24,16},{28,20},{32,56},... | collective-permute-start | bytes 393224 | tf_op jit(solution)/shard_map/ppermute | solution.py:201
  4.1 6.7 %collective-permute-start = (bf16[512,128]{1,0:T(8,128)(2,1)}, bf16[512,128]{1,0:T(8,128)(2,1)S(1)}, u32[]{:S(2)}, u32[]{:S(2)}) collective-permute-start(bf16[512,128]{1,0:T(8,128)(2,1)} %k_ref.1), channel_id=1, source_target_pairs={{0,32},{4,36},{8,40},{12,44},{16,48},{20,52},{24,56},{28,60},{32,6... | collective-permute-start | bytes 393224 | tf_op jit(solution)/shard_map/ppermute | solution.py:201
  5.8 6.0 %collective-permute-start.2 = (bf16[512,128]{1,0:T(8,128)(2,1)}, bf16[512,128]{1,0:T(8,128)(2,1)S(1)}, u32[]{:S(2)}, u32[]{:S(2)}) collective-permute-start(bf16[512,128]{1,0:T(8,128)(2,1)} %k_ref.1), channel_id=1, source_target_pairs={{0,96},{4,100},{8,104},{12,108},{16,112},{20,116},{24,120},{28,124... | collective-permute-start | bytes 393224 | tf_op jit(solution)/shard_map/ppermute | solution.py:201
  8.0 6.0 %collective-permute-start.9 = (bf16[256,128]{1,0:T(8,128)(2,1)S(1)}, bf16[256,128]{1,0:T(8,128)(2,1)S(1)}, u32[]{:S(2)}, u32[]{:S(2)}) collective-permute-start(bf16[256,128]{1,0:T(8,128)(2,1)S(1)} %slice.60), channel_id=1, source_target_pairs={{0,8},{4,12},{8,16},{12,20},{16,24},{20,28},{24,0},{28,4},{32,40},... | collective-permute-start | bytes 196616 | tf_op jit(solution)/shard_map/ppermute | solution.py:201
  8.1 5.9 %collective-permute-start.11 = (bf16[256,128]{1,0:T(8,128)(2,1)S(1)}, bf16[256,128]{1,0:T(8,128)(2,1)S(1)}, u32[]{:S(2)}, u32[]{:S(2)}) collective-permute-start(bf16[256,128]{1,0:T(8,128)(2,1)S(1)} %slice.61), channel_id=1, source_target_pairs={{0,24},{4,28},{8,0},{12,4},{16,8},{20,12},{24,16},{28,20},{32,56},... | collective-permute-start | bytes 196616 | tf_op jit(solution)/shard_map/ppermute | solution.py:201
  10.8 5.8 %collective-permute-start.1 = (bf16[256,128]{1,0:T(8,128)(2,1)S(1)}, bf16[256,128]{1,0:T(8,128)(2,1)S(1)}, u32[]{:S(2)}, u32[]{:S(2)}) collective-permute-start(bf16[256,128]{1,0:T(8,128)(2,1)S(1)} %slice.56), channel_id=1, source_target_pairs={{0,32},{4,36},{8,40},{12,44},{16,48},{20,52},{24,56},{28,60},{32,6... | collective-permute-start | bytes 196616 | tf_op jit(solution)/shard_map/ppermute | solution.py:201
  11.8 4.8 %collective-permute-start.3 = (bf16[256,128]{1,0:T(8,128)(2,1)S(1)}, bf16[256,128]{1,0:T(8,128)(2,1)S(1)}, u32[]{:S(2)}, u32[]{:S(2)}) collective-permute-start(bf16[256,128]{1,0:T(8,128)(2,1)S(1)} %slice.57), channel_id=1, source_target_pairs={{0,96},{4,100},{8,104},{12,108},{16,112},{20,116},{24,120},{28,124... | collective-permute-start | bytes 196616 | tf_op jit(solution)/shard_map/ppermute | solution.py:201
  15.0 25.4 %copy-start.2 = (bf16[4,512,128]{2,1,0:T(8,128)(2,1)}, bf16[4,512,128]{2,1,0:T(8,128)(2,1)S(1)}, u32[]{:S(2)}) copy-start(bf16[4,512,128]{2,1,0:T(8,128)(2,1)S(1)} %pad_maximum_fusion.1.refs_5_) | copy-start | bytes 1572868
  15.0 11.7 %collective-permute-start.14 = (bf16[4,512,128]{2,1,0:T(8,128)(2,1)S(1)}, bf16[4,512,128]{2,1,0:T(8,128)(2,1)S(1)}, u32[]{:S(2)}, u32[]{:S(2)}) collective-permute-start(bf16[4,512,128]{2,1,0:T(8,128)(2,1)S(1)} %pad_maximum_fusion.1.refs_5_), channel_id=1, source_target_pairs={{0,96},{4,100},{8,104},{12,108},{16,112},{20,116},{24,120},{28,124... | collective-permute-start | bytes 1572872 | tf_op jit(solution)/shard_map/ppermute | solution.py:201
  16.5 13.5 %collective-permute-start.12 = (bf16[4,512,128]{2,1,0:T(8,128)(2,1)S(1)}, bf16[4,512,128]{2,1,0:T(8,128)(2,1)S(1)}, u32[]{:S(2)}, u32[]{:S(2)}) collective-permute-start(bf16[4,512,128]{2,1,0:T(8,128)(2,1)S(1)} %pad_maximum_fusion.1.refs_5_), channel_id=1, source_target_pairs={{0,32},{4,36},{8,40},{12,44},{16,48},{20,52},{24,56},{28,60},{32,6... | collective-permute-start | bytes 1572872 | tf_op jit(solution)/shard_map/ppermute | solution.py:201
  17.6 22.8 %copy-start.3 = (bf16[4,512,128]{2,1,0:T(8,128)(2,1)}, bf16[4,512,128]{2,1,0:T(8,128)(2,1)S(1)}, u32[]{:S(2)}) copy-start(bf16[4,512,128]{2,1,0:T(8,128)(2,1)S(1)} %pad_maximum_fusion.refs_0_) | copy-start | bytes 1572868
  17.6 13.2 %collective-permute-start.6 = (bf16[4,512,128]{2,1,0:T(8,128)(2,1)S(1)}, bf16[4,512,128]{2,1,0:T(8,128)(2,1)S(1)}, u32[]{:S(2)}, u32[]{:S(2)}) collective-permute-start(bf16[4,512,128]{2,1,0:T(8,128)(2,1)S(1)} %pad_maximum_fusion.refs_0_), channel_id=1, source_target_pairs={{0,24},{4,28},{8,0},{12,4},{16,8},{20,12},{24,16},{28,20},{32,56},... | collective-permute-start | bytes 1572872 | tf_op jit(solution)/shard_map/ppermute | solution.py:201
  20.3 12.2 %collective-permute-start.4 = (bf16[4,512,128]{2,1,0:T(8,128)(2,1)S(1)}, bf16[4,512,128]{2,1,0:T(8,128)(2,1)S(1)}, u32[]{:S(2)}, u32[]{:S(2)}) collective-permute-start(bf16[4,512,128]{2,1,0:T(8,128)(2,1)S(1)} %pad_maximum_fusion.refs_0_), channel_id=1, source_target_pairs={{0,8},{4,12},{8,16},{12,20},{16,24},{20,28},{24,0},{28,4},{32,40},... | collective-permute-start | bytes 1572872 | tf_op jit(solution)/shard_map/ppermute | solution.py:201
  26.8 13.6 %copy-start.4 = (bf16[4,512,128]{2,1,0:T(8,128)(2,1)}, bf16[4,512,128]{2,1,0:T(8,128)(2,1)S(1)}, u32[]{:S(2)}) copy-start(bf16[4,512,128]{2,1,0:T(8,128)(2,1)S(1)} %collective-permute-done.14.refs_8_) | copy-start | bytes 1572868
  26.8 7.0 %collective-permute-start.15 = (bf16[2,512,128]{2,1,0:T(8,128)(2,1)S(1)}, bf16[2,512,128]{2,1,0:T(8,128)(2,1)}, u32[]{:S(2)}, u32[]{:S(2)}) collective-permute-start(bf16[2,512,128]{2,1,0:T(8,128)(2,1)S(1)} %slice.63), channel_id=1, source_target_pairs={{0,96},{4,100},{8,104},{12,108},{16,112},{20,116},{24,120},{28,124... | collective-permute-start | bytes 786440 | tf_op jit(solution)/shard_map/ppermute | solution.py:201
  30.0 10.4 %copy-start.5 = (bf16[4,512,128]{2,1,0:T(8,128)(2,1)}, bf16[4,512,128]{2,1,0:T(8,128)(2,1)S(1)}, u32[]{:S(2)}) copy-start(bf16[4,512,128]{2,1,0:T(8,128)(2,1)S(1)} %collective-permute-done.12.refs_6_) | copy-start | bytes 1572868
  30.8 6.7 %collective-permute-start.13 = (bf16[2,512,128]{2,1,0:T(8,128)(2,1)}, bf16[2,512,128]{2,1,0:T(8,128)(2,1)}, u32[]{:S(2)}, u32[]{:S(2)}) collective-permute-start(bf16[2,512,128]{2,1,0:T(8,128)(2,1)} %slice.62), channel_id=1, source_target_pairs={{0,32},{4,36},{8,40},{12,44},{16,48},{20,52},{24,56},{28,60},{32,6... | collective-permute-start | bytes 786440 | tf_op jit(solution)/shard_map/ppermute | solution.py:201
  30.8 9.6 %copy-start.6 = (bf16[4,512,128]{2,1,0:T(8,128)(2,1)}, bf16[4,512,128]{2,1,0:T(8,128)(2,1)S(1)}, u32[]{:S(2)}) copy-start(bf16[4,512,128]{2,1,0:T(8,128)(2,1)S(1)} %collective-permute-done.6.refs_3_) | copy-start | bytes 1572868
  31.6 5.9 %collective-permute-start.7 = (bf16[2,512,128]{2,1,0:T(8,128)(2,1)}, bf16[2,512,128]{2,1,0:T(8,128)(2,1)}, u32[]{:S(2)}, u32[]{:S(2)}) collective-permute-start(bf16[2,512,128]{2,1,0:T(8,128)(2,1)} %slice.59), channel_id=1, source_target_pairs={{0,24},{4,28},{8,0},{12,4},{16,8},{20,12},{24,16},{28,20},{32,56},... | collective-permute-start | bytes 786440 | tf_op jit(solution)/shard_map/ppermute | solution.py:201
  33.3 7.0 %collective-permute-start.5 = (bf16[2,512,128]{2,1,0:T(8,128)(2,1)}, bf16[2,512,128]{2,1,0:T(8,128)(2,1)}, u32[]{:S(2)}, u32[]{:S(2)}) collective-permute-start(bf16[2,512,128]{2,1,0:T(8,128)(2,1)} %slice.58), channel_id=1, source_target_pairs={{0,8},{4,12},{8,16},{12,20},{16,24},{20,28},{24,0},{28,4},{32,40},... | collective-permute-start | bytes 786440 | tf_op jit(solution)/shard_map/ppermute | solution.py:201
  66.1 15.7 %collective-permute-start.16 = (bf16[2,3,512,128]{3,2,1,0:T(8,128)(2,1)}, bf16[2,3,512,128]{3,2,1,0:T(8,128)(2,1)S(1)}, u32[]{:S(2)}, u32[]{:S(2)}) collective-permute-start(bf16[2,3,512,128]{3,2,1,0:T(8,128)(2,1)} %pick.1.mine_ref), channel_id=1, source_target_pairs={{0,4},{4,0},{8,12},{12,8},{16,20},{20,16},{24,28},{28,24},{32,36},... | collective-permute-start | bytes 2359304 | tf_op jit(solution)/shard_map/ppermute | solution.py:413
  92.0 21.9 %collective-permute-start.17 = (bf16[128,1024]{1,0:T(8,128)(2,1)S(1)}, bf16[128,1024]{1,0:T(8,128)(2,1)S(1)}, u32[]{:S(2)}, u32[]{:S(2)}) collective-permute-start(bf16[128,1024]{1,0:T(8,128)(2,1)S(1)} %get-tuple-element.17), channel_id=1, source_target_pairs={{0,1},{1,2},{2,3},{3,0},{4,5},{5,6},{6,7},{7,4},{8,9},{9,10},{10,1... | collective-permute-start | bytes 786440 | tf_op jit(solution)/shard_map/ppermute | solution.py:423
  103.1 17.0 %copy-start.1 = (bf16[128,2048]{1,0:T(8,128)(2,1)S(1)}, bf16[128,2048]{1,0:T(8,128)(2,1)}, u32[]{:S(2)}) copy-start(bf16[128,2048]{1,0:T(8,128)(2,1)} %far_attention.7) | copy-start | bytes 1572868
  103.1 17.1 %slice-start = ((bf16[128,2048]{1,0:T(8,128)(2,1)}), bf16[128,1024]{1,0:T(8,128)(2,1)S(1)}, s32[]{:S(2)}) async-start(bf16[128,2048]{1,0:T(8,128)(2,1)} %far_attention.7), calls=%async_computation.4 | async-start | bytes 524288 | tf_op jit(solution)/shard_map/slice | solution.py:432
  112.4 7.6 %collective-permute-start.19 = (bf16[128,1024]{1,0:T(8,128)(2,1)S(1)}, bf16[128,1024]{1,0:T(8,128)(2,1)S(1)}, u32[]{:S(2)}, u32[]{:S(2)}) collective-permute-start(bf16[128,1024]{1,0:T(8,128)(2,1)S(1)} %get-tuple-element.16), channel_id=1, source_target_pairs={{0,3},{1,0},{2,1},{3,2},{4,7},{5,4},{6,5},{7,6},{8,11},{9,8},{10,9... | collective-permute-start | bytes 786440 | tf_op jit(solution)/shard_map/ppermute | solution.py:423
  115.0 21.0 %collective-permute-start.18 = (bf16[128,2048]{1,0:T(8,128)(2,1)S(1)}, bf16[128,2048]{1,0:T(8,128)(2,1)S(1)}, u32[]{:S(2)}, u32[]{:S(2)}) collective-permute-start(bf16[128,2048]{1,0:T(8,128)(2,1)S(1)} %pad_maximum_fusion.2), channel_id=1, source_target_pairs={{0,1},{1,2},{2,3},{3,0},{4,5},{5,6},{6,7},{7,4},{8,9},{9,10},{10,1... | collective-permute-start | bytes 1572872 | tf_op jit(solution)/shard_map/ppermute | solution.py:423
  120.2 15.8 %collective-permute-start.20 = (bf16[128,2048]{1,0:T(8,128)(2,1)S(1)}, bf16[128,2048]{1,0:T(8,128)(2,1)S(1)}, u32[]{:S(2)}, u32[]{:S(2)}) collective-permute-start(bf16[128,2048]{1,0:T(8,128)(2,1)S(1)} %pad_maximum_fusion.3), channel_id=1, source_target_pairs={{0,3},{1,0},{2,1},{3,2},{4,7},{5,4},{6,5},{7,6},{8,11},{9,8},{10,9... | collective-permute-start | bytes 1572872 | tf_op jit(solution)/shard_map/ppermute | solution.py:423
  142.7 59.8 %all-to-all-start.2 = ((bf16[128,8,2048]{2,1,0:T(8,128)(2,1)}), bf16[128,8,2048]{2,1,0:T(8,128)(2,1)}, u32[]{:S(2)}, u32[]{:S(2)}) async-start(bf16[128,8,2048]{2,1,0:T(8,128)(2,1)} %bitcast.29), calls=%async_computation.2 | async-start | bytes 8388608 | tf_op jit(solution)/shard_map/all_to_all | solution.py:436
  202.5 57.4 %all-to-all-start = ((bf16[128,8,2048]{2,1,0:T(8,128)(2,1)}), bf16[128,8,2048]{2,1,0:T(8,128)(2,1)}, u32[]{:S(2)}, u32[]{:S(2)}) async-start(bf16[128,8,2048]{2,1,0:T(8,128)(2,1)} %bitcast.28), calls=%async_computation | async-start | bytes 8388608 | tf_op jit(solution)/shard_map/all_to_all | solution.py:436
  259.9 57.4 %all-to-all-start.3 = ((bf16[128,8,2048]{2,1,0:T(8,128)(2,1)}), bf16[128,8,2048]{2,1,0:T(8,128)(2,1)}, u32[]{:S(2)}, u32[]{:S(2)}) async-start(bf16[128,8,2048]{2,1,0:T(8,128)(2,1)} %bitcast.27), calls=%async_computation.3 | async-start | bytes 8388608 | tf_op jit(solution)/shard_map/all_to_all | solution.py:436
  317.3 57.4 %all-to-all-start.1 = ((bf16[128,8,2048]{2,1,0:T(8,128)(2,1)}), bf16[128,8,2048]{2,1,0:T(8,128)(2,1)}, u32[]{:S(2)}, u32[]{:S(2)}) async-start(bf16[128,8,2048]{2,1,0:T(8,128)(2,1)} %bitcast.26), calls=%async_computation.1 | async-start | bytes 8388608 | tf_op jit(solution)/shard_map/all_to_all | solution.py:436
  (4 other events, 10.5 us)

commit v3 on v1

v3 whole, which is shorter than its diff:
```python
import functools
import math

import jax
import jax.numpy as jnp
from jax import lax
from jax.experimental import pallas as pl
from jax.experimental.pallas import tpu as pltpu
from jax.sharding import PartitionSpec as P

HD = 128
FFE = 768
TOP = 8
BLK = 128
DIST = 3
CAP = 16
CHUNKS = 2
PAIR = 2
ALL = ("ctx", "head")
BF16 = jnp.bfloat16
F32 = jnp.float32
NT = (((1,), (1,)), ((), ()))
TN = (((0,), (0,)), ((), ()))
EXPONENT = math.log2(math.e) / math.sqrt(HD)
VMEM_LIMIT = 56 * 1024 * 1024


def params(steps=1):
    return pltpu.CompilerParams(
        dimension_semantics=("arbitrary",) * steps, vmem_limit_bytes=VMEM_LIMIT
    )


def attention_kernel(
    place, wanted, q_ref, k_ref, v_ref, far0_ref, far1_ref, far2_ref, w_ref, *refs
):
    out_refs, mixed_ref = refs[:-1], refs[-1]
    step = pl.program_id(0)
    blocks = k_ref.shape[0] // BLK
    heads = q_ref.shape[1] // HD
    block = lax.rem(place[0] + step, blocks)
    far_refs = (far0_ref, far1_ref, far2_ref)

    def attend(at):
        near = at * BLK
        later = lax.broadcasted_iota(jnp.int32, (BLK, BLK), 0) > lax.broadcasted_iota(
            jnp.int32, (BLK, BLK), 1
        )
        bias = jnp.where(later, -jnp.inf, 0.0)
        bias = jnp.concatenate([bias] * PAIR, axis=1)
        reach = [jnp.where(place[1] >= wanted[0, j], 0.0, -jnp.inf) for j in range(DIST)]
        keys = jnp.concatenate([k_ref[: near + BLK]] + [r[0] for r in far_refs], axis=0)
        values = jnp.concatenate([v_ref[: near + BLK]] + [r[1] for r in far_refs], axis=0)
        for n in range(0, heads, PAIR):
            query = jnp.concatenate(
                [q_ref[:, (n + i) * HD : (n + i + 1) * HD] for i in range(PAIR)], axis=0
            )
            score = lax.dot_general(keys, query, NT, preferred_element_type=F32)
            parts = [score[:near]] if at else []
            parts.append(score[near : near + BLK] + bias)
            for j in range(DIST):
                start = near + (j + 1) * BLK
                parts.append(score[start : start + BLK] + reach[j])
            score = jnp.concatenate(parts, axis=0)
            highest = jnp.max(score, axis=0, keepdims=True)
            weight = jnp.exp2((score - highest) * EXPONENT)
            denominator = jnp.sum(weight, axis=0, keepdims=True)
            mixed = lax.dot_general(values, weight.astype(BF16), TN, preferred_element_type=F32)
            mixed = mixed / denominator
            for i in range(PAIR):
                mixed_ref[pl.ds(step * BLK, BLK), (n + i) * HD : (n + i + 1) * HD] = (
                    mixed[:, i * BLK : (i + 1) * BLK].T.astype(BF16)
                )

    for at in range(blocks):
        pl.when(block == at)(functools.partial(attend, at))

    @pl.when(step == blocks - 1)
    def _():
        for i, out_ref in enumerate(out_refs):
            out_ref[...] = jnp.dot(
                mixed_ref[i * BLK : (i + 1) * BLK], w_ref[...], preferred_element_type=F32
            ).astype(BF16)


def attention(place, wanted, queries, keys, values, far, out_weight):
    length, wide = queries.shape
    width = out_weight.shape[1]
    blocks = length // BLK
    at = lambda i, place: lax.rem(place[0] + i, blocks)
    whole = lambda shape: pl.BlockSpec(
        shape, lambda i, p, w: (0,) * len(shape), pipeline_mode=pl.Buffered(1)
    )
    return pl.pallas_call(
        attention_kernel,
        grid_spec=pltpu.PrefetchScalarGridSpec(
            num_scalar_prefetch=2,
            grid=(blocks,),
            in_specs=[
                pl.BlockSpec((BLK, wide), lambda i, p, w: (at(i, p), 0)),
                whole(keys.shape),
                whole(values.shape),
            ]
            + [pl.BlockSpec((2, BLK, HD), lambda i, p, w: (0, at(i, p), 0))] * DIST
            + [whole(out_weight.shape)],
            out_specs=(whole((BLK, width)),) * blocks,
            scratch_shapes=[pltpu.VMEM((length, wide), BF16)],
        ),
        out_shape=(jax.ShapeDtypeStruct((BLK, width), BF16),) * blocks,
        compiler_params=params(),
        name="attention",
    )(place, wanted, queries, keys, values, *far, out_weight)


def tables_kernel(routes_ref, weights_ref, send_ref, table_ref, spread_ref):
    top, tokens = routes_ref.shape
    experts, slots = spread_ref.shape[:2]
    chunks = send_ref.shape[0]
    names = lax.broadcasted_iota(jnp.int32, (experts, tokens), 0)
    chosen = jnp.zeros((experts, tokens), F32)
    weight = jnp.zeros((experts, tokens), F32)
    for k in range(top):
        here = routes_ref[k : k + 1, :] == names
        chosen = jnp.where(here, 1.0, chosen)
        weight = jnp.where(here, weights_ref[k : k + 1, :], weight)
    before = (
        lax.broadcasted_iota(jnp.int32, (tokens, tokens), 0)
        < lax.broadcasted_iota(jnp.int32, (tokens, tokens), 1)
    ).astype(BF16)
    place = jnp.dot(chosen.astype(BF16), before, preferred_element_type=F32)
    place = jnp.where(chosen > 0.0, place, -1.0)
    high = weight.astype(BF16).astype(F32)
    low = weight - high

    def spread(c, value):
        for s in range(slots):
            spread_ref[:, s, :] = jnp.where(place == float(c * slots + s), value, 0.0)
        return spread_ref[...].reshape(experts * slots, tokens).astype(BF16)

    for c in range(chunks):
        send_ref[c] = spread(c, 1.0)
        table_ref[c, :, :tokens] = spread(c, high)
        table_ref[c, :, tokens:] = spread(c, low)


def tables(routes, route_weights, experts):
    tokens = routes.shape[0]
    slots = CAP // CHUNKS
    return pl.pallas_call(
        tables_kernel,
        out_shape=(
            jax.ShapeDtypeStruct((CHUNKS, experts * slots, tokens), BF16),
            jax.ShapeDtypeStruct((CHUNKS, experts * slots, 2 * tokens), BF16),
        ),
        scratch_shapes=[pltpu.VMEM((experts, slots, tokens), F32)],
        compiler_params=params(0),
        name="tables",
    )(routes.T, route_weights.T)


def norm_kernel(
    own_ref, r1_ref, r2_ref, r3_ref, residual_ref, gain_ref, send_ref, attended_ref, normed_ref, out_ref
):
    @pl.when(pl.program_id(0) == 0)
    def _():
        total = residual_ref[...].astype(F32) + own_ref[...].astype(F32)
        for part_ref in (r1_ref, r2_ref, r3_ref):
            total = total + part_ref[...].astype(F32)
        attended = total.astype(BF16)
        attended_ref[...] = attended
        wide = attended.astype(F32)
        inverse = lax.rsqrt(jnp.mean(wide * wide, axis=1, keepdims=True) + 1e-06)
        normed_ref[...] = (wide * inverse * gain_ref[...]).astype(BF16)

    out_ref[...] = jnp.dot(send_ref[0], normed_ref[...], preferred_element_type=F32).astype(BF16)


def norm_dispatch(own, others, residual, gain, send):
    tokens, width = residual.shape
    rows = send.shape[1]
    step = 256
    whole = lambda shape: pl.BlockSpec(shape, lambda i: (0,) * len(shape))
    return pl.pallas_call(
        norm_kernel,
        grid=(rows // step,),
        in_specs=[pl.BlockSpec(memory_space=pltpu.VMEM)] * 4
        + [whole((tokens, width)), whole((1, width)), pl.BlockSpec((1, step, tokens), lambda i: (0, i, 0))],
        out_specs=(
            whole((tokens, width)),
            whole((tokens, width)),
            pl.BlockSpec((step, width), lambda i: (i, 0)),
        ),
        out_shape=(
            jax.ShapeDtypeStruct((tokens, width), BF16),
            jax.ShapeDtypeStruct((tokens, width), BF16),
            jax.ShapeDtypeStruct((rows, width), BF16),
        ),
        compiler_params=params(),
        name="norm_dispatch",
    )(own, *others, residual, gain.reshape(1, width), send)


def dispatch_kernel(send_ref, normed_ref, out_ref):
    out_ref[...] = jnp.dot(send_ref[0], normed_ref[...], preferred_element_type=F32).astype(BF16)


def dispatch(send, normed, chunk):
    tokens, width = normed.shape
    rows = send.shape[1]
    step = 256
    return pl.pallas_call(
        dispatch_kernel,
        grid=(rows // step,),
        in_specs=[
            pl.BlockSpec((1, step, tokens), lambda i: (chunk, i, 0)),
            pl.BlockSpec((tokens, width), lambda i: (0, 0)),
        ],
        out_specs=pl.BlockSpec((step, width), lambda i: (i, 0)),
        out_shape=jax.ShapeDtypeStruct((rows, width), BF16),
        compiler_params=params(),
        name="dispatch",
    )(send, normed)


def expert_kernel(x_ref, gate_up_ref, down_ref, out_ref):
    projected = jnp.dot(x_ref[...], gate_up_ref[0], preferred_element_type=F32)
    gate, up = projected[:, :FFE], projected[:, FFE:]
    hidden = (gate / (1.0 + jnp.exp(-gate)) * up).astype(BF16)
    out_ref[...] = jnp.dot(hidden, down_ref[0], preferred_element_type=F32).astype(BF16)


def expert(x, gate_up, down):
    rows, width = x.shape
    step = 256
    whole = lambda shape: pl.BlockSpec(
        shape, lambda i: (0,) * len(shape), pipeline_mode=pl.Buffered(1)
    )
    return pl.pallas_call(
        expert_kernel,
        grid=(rows // step,),
        in_specs=[
            pl.BlockSpec((step, width), lambda i: (i, 0)),
            whole(gate_up.shape),
            whole(down.shape),
        ],
        out_specs=pl.BlockSpec((step, width), lambda i: (i, 0)),
        out_shape=jax.ShapeDtypeStruct((rows, width), BF16),
        compiler_params=params(),
        name="expert",
    )(x, gate_up, down)


def combine_kernel(table_ref, rows_ref, *refs):
    before_ref, (out_ref, total_ref) = (refs[0] if len(refs) == 3 else None), refs[-2:]
    step = pl.program_id(0)
    tokens = out_ref.shape[0]
    part = lax.dot_general(table_ref[0], rows_ref[...], TN, preferred_element_type=F32)
    part = part[:tokens] + part[tokens:]

    @pl.when(step == 0)
    def _():
        total_ref[...] = part if before_ref is None else part + before_ref[...]

    @pl.when(step > 0)
    def _():
        total_ref[...] += part

    @pl.when(step == pl.num_programs(0) - 1)
    def _():
        out_ref[...] = total_ref[...].astype(out_ref.dtype)


def combine(table, rows, before, dtype, chunk):
    count, width = rows.shape
    tokens = table.shape[2] // 2
    step = 256
    whole = lambda shape: pl.BlockSpec(shape, lambda i: (0,) * len(shape))
    operands = (table, rows) + (() if before is None else (before,))
    return pl.pallas_call(
        combine_kernel,
        grid=(count // step,),
        in_specs=[
            pl.BlockSpec((1, step, 2 * tokens), lambda i: (chunk, i, 0)),
            pl.BlockSpec((step, width), lambda i: (i, 0)),
        ]
        + ([] if before is None else [whole(before.shape)]),
        out_specs=whole((tokens, width)),
        out_shape=jax.ShapeDtypeStruct((tokens, width), dtype),
        scratch_shapes=[pltpu.VMEM((tokens, width), F32)],
        compiler_params=params(),
        name="combine",
    )(*operands)


def fetch(packed, distance):
    shards = lax.axis_size("ctx")

    def back(by, block):
        return lax.ppermute(block, "ctx", [(i, i + by) for i in range(shards - by)])

    return lax.switch(
        distance - 1, [functools.partial(back, by) for by in range(1, shards)], packed
    )


def body(
    queries,
    keys,
    values,
    distances,
    out_weight,
    residual,
    norm_gain,
    expert_gate_up,
    expert_down,
    routes,
    route_weights,
):
    tokens, width = residual.shape
    devices = lax.axis_size(ALL)
    me, head = lax.axis_index("ctx"), lax.axis_index("head")
    place = jnp.stack([head, me])
    packed = jnp.stack([keys, values])
    far = [fetch(packed, distances[0, j]) for j in range(DIST)]
    send, table = tables(routes, route_weights, devices)
    own, one, two, three = attention(
        place, distances, queries, keys, values, far, out_weight
    )
    others = [
        lax.ppermute(a, "head", [(i, (i + r) % 4) for i in range(4)])
        for a, r in ((two, 2), (one, 1), (three, 3))
    ]
    attended, normed, first = norm_dispatch(own, others, residual, norm_gain, send)
    exchange = lambda a: lax.all_to_all(a, ALL, split_axis=0, concat_axis=0, tiled=True)
    arrived = [exchange(first)]
    for c in range(1, CHUNKS):
        arrived.append(exchange(dispatch(send, normed, c)))
    returned = [exchange(expert(a, expert_gate_up, expert_down)) for a in arrived]
    total = None
    for c in range(CHUNKS):
        total = combine(table, returned[c], total, BF16 if c == CHUNKS - 1 else F32, c)
    return (attended, total)


def solution(mesh):
    return jax.shard_map(
        body,
        mesh=mesh,
        in_specs=(
            P("ctx", "head"),
            P("ctx", "head"),
            P("ctx", "head"),
            P("head", None),
            P("head", None),
            P(ALL, None),
            P(),
            P(ALL, None, None),
            P(ALL, None, None),
            P(ALL, None),
            P(ALL, None),
        ),
        out_specs=(P(ALL, None), P(ALL, None)),
        check_vma=False,
    )
```

time: 370 us -> 334 us (0.903)
  waiting for transfers between devices: 238 us -> 204 us
  starting transfers between devices: 25.5 us -> 46.4 us
  between operations: 19.6 us -> 2.7 us
  other arithmetic: 6.18 us -> 1.58 us
    all_gather x1 -> x0, waiting for transfers between devices: 50.6 us -> none  [body(): everything = lax.all_gather(packed, 'ctx', axis=0, tiled=True)]
    ppermute x0 -> x6, waiting for transfers between devices: none -> 34.4 us  [the longest x3 19.6 us: body(): lax.ppermute(a, 'head', [(i, (i + r) % 4) for i in range(4)])]
    ppermute x0 -> x6, starting transfers between devices: none -> 21.7 us  [the longest x3 19 us: back(): return lax.ppermute(block, 'ctx', [(i, i + by) for i in range(shards - by)])]
    all_to_all x1 -> x0, waiting for transfers between devices: 19.7 us -> none  [body(): lax.all_to_all(projected, 'head', split_axis=0, concat_axis=0, tiled=True)]
    all_to_all x1 -> x0, starting transfers between devices: 4 us -> none  [body(): lax.all_to_all(projected, 'head', split_axis=0, concat_axis=0, tiled=True)]
  transfers between devices with their start and end apart: 6 -> 10, of which waited for: 6 -> 9; matrix products, arithmetic and copies ran while one was open for 2% -> 0% of each run, Pallas kernels for 12% -> 14%
where the time goes in v3:
time: 334 us; the launch traced here: 330 us
  waiting for transfers between devices  204 us (61%)
  Pallas kernels  72.7 us (22%)
  starting transfers between devices  46.4 us (14%)
    all_to_all x4, waiting for transfers between devices, body(): lax.all_to_all(a, ALL, split_axis=0, concat_axis=0, tiled=True)  169 us
    pallas_call x2, Pallas kernels, expert(): pl.pallas_call(expert_kernel, grid=(rows // step,), in_specs=[pl.BlockSpe...  31.1 us
    all_to_all x4, starting transfers between devices, body(): lax.all_to_all(a, ALL, split_axis=0, concat_axis=0, tiled=True)  24.6 us
    ppermute x3, waiting for transfers between devices, body(): lax.ppermute(a, 'head', [(i, (i + r) % 4) for i in range(4)])  19.6 us
    ppermute x3, starting transfers between devices, back(): return lax.ppermute(block, 'ctx', [(i, i + by) for i in range(shards - by)])  19 us
    pallas_call x1, Pallas kernels, attention(): pl.pallas_call(attention_kernel, grid_spec=pltpu.PrefetchScalarGridSpec(n...  16.1 us
    ppermute x3, waiting for transfers between devices, back(): return lax.ppermute(block, 'ctx', [(i, i + by) for i in range(shards - by)])  14.7 us
    pallas_call x2, Pallas kernels, combine(): pl.pallas_call(combine_kernel, grid=(count // step,), in_specs=[pl.BlockS...  10.9 us
  transfers between devices with their start and end apart: 10, of which 9 were waited for; matrix products, arithmetic and copies ran while one was open for 0% of the time, Pallas kernels for 14%

profile of v3, /device:TPU:1, one launch (start us, length us, event | category | flops | bytes accessed | tf_op | source)
XLA Modules:
  0.0 329.6 jit_solution(664885999370597980)
XLA Ops:
  0.6 1.4 fusion
  4.1 1.0 pad_maximum_fusion
  5.1 13.8 %conditional.5 = (bf16[2,512,128]{2,1,0:T(8,128)(2,1)}) conditional(s32[]{:T(128)} %bitcast.6, bf16[2,512,128]{2,1,0:T(8,128)(2,1)S(1)} %pad_maximum_fusion, bf16[2,512,128]{2,1,0:T(8,128)(2,1)S(1)} %pad_maximum_fusion, bf16[2,512,128]{2,1,0:T(8,128)(2,1)S(1)} %pad_maximum_fusion, ...), branch_computations={%region_62.0_spmd, %region_63.0_spmd, %region_64.0_spmd, %region_6... | conditional | bytes 1048624 | solution.py:301
  5.1 9.5 %collective-permute-start.81 = (bf16[2,512,128]{2,1,0:T(8,128)(2,1)S(1)}, bf16[2,512,128]{2,1,0:T(8,128)(2,1)}, u32[]{:S(2)}, u32[]{:S(2)}) collective-permute-start(bf16[2,512,128]{2,1,0:T(8,128)(2,1)S(1)} %param.81), channel_id=1, source_target_pairs={{0,80},{4,84},{8,88},{12,92},{16,96},{20,100},{24,104},{28,108},{3... | collective-permute-start | bytes 786440 | tf_op jit(solution)/shard_map/cond/branch_19_fun/ppermute | solution.py:299
  14.6 4.2 %collective-permute-done.81 = bf16[2,512,128]{2,1,0:T(8,128)(2,1)} collective-permute-done((bf16[2,512,128]{2,1,0:T(8,128)(2,1)S(1)}, bf16[2,512,128]{2,1,0:T(8,128)(2,1)}, u32[]{:S(2)}, u32[]{:S(2)}) %collective-permute-start.81) | collective-permute-done | bytes 262176 | tf_op jit(solution)/shard_map/cond/branch_19_fun/ppermute | solution.py:299
  18.8 10.2 %conditional.4 = (bf16[2,512,128]{2,1,0:T(8,128)(2,1)}) conditional(s32[]{:T(128)} %bitcast.5, bf16[2,512,128]{2,1,0:T(8,128)(2,1)S(1)} %pad_maximum_fusion, bf16[2,512,128]{2,1,0:T(8,128)(2,1)S(1)} %pad_maximum_fusion, bf16[2,512,128]{2,1,0:T(8,128)(2,1)S(1)} %pad_maximum_fusion, ...), branch_computations={%region_31.0_spmd, %region_32.0_spmd, %region_33.0_spmd, %region_3... | conditional | bytes 1048624 | solution.py:301
  18.8 4.8 %collective-permute-start.37 = (bf16[2,512,128]{2,1,0:T(8,128)(2,1)S(1)}, bf16[2,512,128]{2,1,0:T(8,128)(2,1)}, u32[]{:S(2)}, u32[]{:S(2)}) collective-permute-start(bf16[2,512,128]{2,1,0:T(8,128)(2,1)S(1)} %param.37), channel_id=1, source_target_pairs={{0,28},{4,32},{8,36},{12,40},{16,44},{20,48},{24,52},{28,56},{32,6... | collective-permute-start | bytes 786440 | tf_op jit(solution)/shard_map/cond/branch_6_fun/ppermute | solution.py:299
  23.6 5.4 %collective-permute-done.37 = bf16[2,512,128]{2,1,0:T(8,128)(2,1)} collective-permute-done((bf16[2,512,128]{2,1,0:T(8,128)(2,1)S(1)}, bf16[2,512,128]{2,1,0:T(8,128)(2,1)}, u32[]{:S(2)}, u32[]{:S(2)}) %collective-permute-start.37) | collective-permute-done | bytes 262176 | tf_op jit(solution)/shard_map/cond/branch_6_fun/ppermute | solution.py:299
  29.0 9.8 %conditional.3 = (bf16[2,512,128]{2,1,0:T(8,128)(2,1)}) conditional(s32[]{:T(128)} %bitcast.2, bf16[2,512,128]{2,1,0:T(8,128)(2,1)S(1)} %pad_maximum_fusion, bf16[2,512,128]{2,1,0:T(8,128)(2,1)S(1)} %pad_maximum_fusion, bf16[2,512,128]{2,1,0:T(8,128)(2,1)S(1)} %pad_maximum_fusion, ...), branch_computations={%region_0.0_spmd, %region_1.0_spmd, %region_2.0_spmd, %region_3.0_... | conditional | bytes 1048624 | solution.py:301
  29.0 4.7 %collective-permute-start.13 = (bf16[2,512,128]{2,1,0:T(8,128)(2,1)S(1)}, bf16[2,512,128]{2,1,0:T(8,128)(2,1)}, u32[]{:S(2)}, u32[]{:S(2)}) collective-permute-start(bf16[2,512,128]{2,1,0:T(8,128)(2,1)S(1)} %param.13), channel_id=1, source_target_pairs={{0,56},{4,60},{8,64},{12,68},{16,72},{20,76},{24,80},{28,84},{32,8... | collective-permute-start | bytes 786440 | tf_op jit(solution)/shard_map/cond/branch_13_fun/ppermute | solution.py:299
  33.7 5.1 %collective-permute-done.13 = bf16[2,512,128]{2,1,0:T(8,128)(2,1)} collective-permute-done((bf16[2,512,128]{2,1,0:T(8,128)(2,1)S(1)}, bf16[2,512,128]{2,1,0:T(8,128)(2,1)}, u32[]{:S(2)}, u32[]{:S(2)}) %collective-permute-start.13) | collective-permute-done | bytes 262176 | tf_op jit(solution)/shard_map/cond/branch_13_fun/ppermute | solution.py:299
  38.8 0.6 pad_add_fusion.place
  39.4 16.1 %attention.1 = (bf16[128,2048]{1,0:T(8,128)(2,1)}, bf16[128,2048]{1,0:T(8,128)(2,1)}, bf16[128,2048]{1,0:T(8,128)(2,1)}, bf16[128,2048]{1,0:T(8,128)(2,1)}) custom-call(s32[2]{0:T(128)} %pad_add_fusion.place, s32[1,3]{1,0:T(1,128)} %wanted.1, bf16[512,1024]{1,0:T(8,128)(2,1)} %q_ref.1, bf16[512,128]{1,0:T(8,128)(2,1)} %k_ref.1, bf16[512,128]{1,0:T(8,128)(2,1)} %v_ref.1, ...), custom_call_target="tpu_custom_call" | custom-call | tf_op jit(solution)/shard_map/attention/pallas_call | solution.py:94
  55.6 2.7 collective-permute-start.95
  58.3 4.0 %tables.1 = (bf16[2,1024,128]{2,1,0:T(8,128)(2,1)}, bf16[2,1024,256]{2,1,0:T(8,128)(2,1)}) custom-call(s32[8,128]{1,0:T(8,128)} %bitcast.25, f32[8,128]{1,0:T(8,128)} %bitcast.26), custom_call_target="tpu_custom_call" | custom-call | tf_op jit(solution)/shard_map/tables/pallas_call | solution.py:149
  62.3 7.8 %collective-permute-done.93.r1_ref = bf16[128,2048]{1,0:T(8,128)(2,1)S(1)} collective-permute-done((bf16[128,2048]{1,0:T(8,128)(2,1)}, bf16[128,2048]{1,0:T(8,128)(2,1)S(1)}, u32[]{:S(2)}, u32[]{:S(2)}) %collective-permute-start.93) | collective-permute-done | bytes 524320 | tf_op jit(solution)/shard_map/ppermute | solution.py:330
  70.1 11.8 %collective-permute-done.94.r2_ref = bf16[128,2048]{1,0:T(8,128)(2,1)S(1)} collective-permute-done((bf16[128,2048]{1,0:T(8,128)(2,1)}, bf16[128,2048]{1,0:T(8,128)(2,1)S(1)}, u32[]{:S(2)}, u32[]{:S(2)}) %collective-permute-start.94) | collective-permute-done | bytes 524320 | tf_op jit(solution)/shard_map/ppermute | solution.py:330
  81.9 0.8 copy-done.1
  82.9 5.9 %norm_dispatch.1 = (bf16[128,2048]{1,0:T(8,128)(2,1)}, bf16[128,2048]{1,0:T(8,128)(2,1)}, bf16[1024,2048]{1,0:T(8,128)(2,1)}) custom-call(bf16[128,2048]{1,0:T(8,128)(2,1)} %get-tuple-element.200.own_ref, bf16[128,2048]{1,0:T(8,128)(2,1)} %copy-done, bf16[128,2048]{1,0:T(8,128)(2,1)} %copy-done.1, bf16[128,2048]{1,0:T(8,128)(2,1)} %copy-done.2, ...), custom_call_target="tpu_custom_call" | custom-call | tf_op jit(solution)/shard_map/norm_dispatch/pallas_call | solution.py:183
  88.8 10.4 %all-to-all-start.2 = ((bf16[128,8,2048]{2,1,0:T(8,128)(2,1)}), bf16[128,8,2048]{2,1,0:T(8,128)(2,1)}, u32[]{:S(2)}, u32[]{:S(2)}) async-start(bf16[128,8,2048]{2,1,0:T(8,128)(2,1)} %bitcast.21), calls=%async_computation.2 | async-start | bytes 8388608 | tf_op jit(solution)/shard_map/all_to_all | solution.py:334
  99.2 4.7 %dispatch.1 = bf16[1024,2048]{1,0:T(8,128)(2,1)} custom-call(bf16[2,1024,128]{2,1,0:T(8,128)(2,1)} %get-tuple-element.204.send_ref, bf16[128,2048]{1,0:T(8,128)(2,1)} %get-tuple-element.207.normed_ref), custom_call_target="tpu_custom_call" | custom-call | tf_op jit(solution)/shard_map/dispatch/pallas_call | solution.py:211
  103.9 48.1 %all-to-all-done.2 = bf16[128,8,2048]{2,1,0:T(8,128)(2,1)} async-done(((bf16[128,8,2048]{2,1,0:T(8,128)(2,1)}), bf16[128,8,2048]{2,1,0:T(8,128)(2,1)}, u32[]{:S(2)}, u32[]{:S(2)}) %all-to-all-start.2) | async-done | bytes 4194336 | tf_op jit(solution)/shard_map/all_to_all | solution.py:334
  152.1 4.8 %all-to-all-start = ((bf16[128,8,2048]{2,1,0:T(8,128)(2,1)}), bf16[128,8,2048]{2,1,0:T(8,128)(2,1)}, u32[]{:S(2)}, u32[]{:S(2)}) async-start(bf16[128,8,2048]{2,1,0:T(8,128)(2,1)} %bitcast.20), calls=%async_computation | async-start | bytes 8388608 | tf_op jit(solution)/shard_map/all_to_all | solution.py:334
  156.8 15.5 %expert.3 = bf16[1024,2048]{1,0:T(8,128)(2,1)} custom-call(bf16[1024,2048]{1,0:T(8,128)(2,1)} %bitcast.15.x_ref, bf16[1,2048,1536]{2,1,0:T(8,128)(2,1)} %gate_up_ref.3, bf16[1,768,2048]{2,1,0:T(8,128)(2,1)} %down_ref.3), custom_call_target="tpu_custom_call" | custom-call | tf_op jit(solution)/shard_map/expert/pallas_call | solution.py:238
  172.4 37.0 %all-to-all-done = bf16[128,8,2048]{2,1,0:T(8,128)(2,1)} async-done(((bf16[128,8,2048]{2,1,0:T(8,128)(2,1)}), bf16[128,8,2048]{2,1,0:T(8,128)(2,1)}, u32[]{:S(2)}, u32[]{:S(2)}) %all-to-all-start) | async-done | bytes 4194336 | tf_op jit(solution)/shard_map/all_to_all | solution.py:334
  209.4 4.8 %all-to-all-start.3 = ((bf16[128,8,2048]{2,1,0:T(8,128)(2,1)}), bf16[128,8,2048]{2,1,0:T(8,128)(2,1)}, u32[]{:S(2)}, u32[]{:S(2)}) async-start(bf16[128,8,2048]{2,1,0:T(8,128)(2,1)} %bitcast.19), calls=%async_computation.3 | async-start | bytes 8388608 | tf_op jit(solution)/shard_map/all_to_all | solution.py:334
  214.2 15.5 %expert.2 = bf16[1024,2048]{1,0:T(8,128)(2,1)} custom-call(bf16[1024,2048]{1,0:T(8,128)(2,1)} %bitcast.11.x_ref, bf16[1,2048,1536]{2,1,0:T(8,128)(2,1)} %gate_up_ref.3, bf16[1,768,2048]{2,1,0:T(8,128)(2,1)} %down_ref.3), custom_call_target="tpu_custom_call" | custom-call | tf_op jit(solution)/shard_map/expert/pallas_call | solution.py:238
  229.7 37.1 %all-to-all-done.3 = bf16[128,8,2048]{2,1,0:T(8,128)(2,1)} async-done(((bf16[128,8,2048]{2,1,0:T(8,128)(2,1)}), bf16[128,8,2048]{2,1,0:T(8,128)(2,1)}, u32[]{:S(2)}, u32[]{:S(2)}) %all-to-all-start.3) | async-done | bytes 4194336 | tf_op jit(solution)/shard_map/all_to_all | solution.py:334
  266.8 4.8 %all-to-all-start.1 = ((bf16[128,8,2048]{2,1,0:T(8,128)(2,1)}), bf16[128,8,2048]{2,1,0:T(8,128)(2,1)}, u32[]{:S(2)}, u32[]{:S(2)}) async-start(bf16[128,8,2048]{2,1,0:T(8,128)(2,1)} %bitcast.18), calls=%async_computation.1 | async-start | bytes 8388608 | tf_op jit(solution)/shard_map/all_to_all | solution.py:334
  271.5 5.4 %combine.2.refs_0_ = f32[128,2048]{1,0:T(8,128)} custom-call(bf16[2,1024,256]{2,1,0:T(8,128)(2,1)} %get-tuple-element.206.table_ref, bf16[1024,2048]{1,0:T(8,128)(2,1)} %bitcast.17.rows_ref), custom_call_target="tpu_custom_call" | custom-call | tf_op jit(solution)/shard_map/combine/pallas_call | solution.py:279
  276.9 47.2 %all-to-all-done.1 = bf16[128,8,2048]{2,1,0:T(8,128)(2,1)} async-done(((bf16[128,8,2048]{2,1,0:T(8,128)(2,1)}), bf16[128,8,2048]{2,1,0:T(8,128)(2,1)}, u32[]{:S(2)}, u32[]{:S(2)}) %all-to-all-start.1) | async-done | bytes 4194336 | tf_op jit(solution)/shard_map/all_to_all | solution.py:334
  324.1 5.5 %combine.3 = bf16[128,2048]{1,0:T(8,128)(2,1)} custom-call(bf16[2,1024,256]{2,1,0:T(8,128)(2,1)} %get-tuple-element.206.table_ref, bf16[1024,2048]{1,0:T(8,128)(2,1)} %bitcast.13.rows_ref, f32[128,2048]{1,0:T(8,128)} %combine.2.refs_0_), custom_call_target="tpu_custom_call" | custom-call | tf_op jit(solution)/shard_map/combine/pallas_call | solution.py:279
  (8 shorter events, 0.2 us)
Async XLA Ops:
  5.1 13.8 %collective-permute-start.81 = (bf16[2,512,128]{2,1,0:T(8,128)(2,1)S(1)}, bf16[2,512,128]{2,1,0:T(8,128)(2,1)}, u32[]{:S(2)}, u32[]{:S(2)}) collective-permute-start(bf16[2,512,128]{2,1,0:T(8,128)(2,1)S(1)} %param.81), channel_id=1, source_target_pairs={{0,80},{4,84},{8,88},{12,92},{16,96},{20,100},{24,104},{28,108},{3... | collective-permute-start | bytes 786440 | tf_op jit(solution)/shard_map/cond/branch_19_fun/ppermute | solution.py:299
  18.8 10.2 %collective-permute-start.37 = (bf16[2,512,128]{2,1,0:T(8,128)(2,1)S(1)}, bf16[2,512,128]{2,1,0:T(8,128)(2,1)}, u32[]{:S(2)}, u32[]{:S(2)}) collective-permute-start(bf16[2,512,128]{2,1,0:T(8,128)(2,1)S(1)} %param.37), channel_id=1, source_target_pairs={{0,28},{4,32},{8,36},{12,40},{16,44},{20,48},{24,52},{28,56},{32,6... | collective-permute-start | bytes 786440 | tf_op jit(solution)/shard_map/cond/branch_6_fun/ppermute | solution.py:299
  29.0 9.8 %collective-permute-start.13 = (bf16[2,512,128]{2,1,0:T(8,128)(2,1)S(1)}, bf16[2,512,128]{2,1,0:T(8,128)(2,1)}, u32[]{:S(2)}, u32[]{:S(2)}) collective-permute-start(bf16[2,512,128]{2,1,0:T(8,128)(2,1)S(1)} %param.13), channel_id=1, source_target_pairs={{0,56},{4,60},{8,64},{12,68},{16,72},{20,76},{24,80},{28,84},{32,8... | collective-permute-start | bytes 786440 | tf_op jit(solution)/shard_map/cond/branch_13_fun/ppermute | solution.py:299
  55.6 14.6 %collective-permute-start.93 = (bf16[128,2048]{1,0:T(8,128)(2,1)}, bf16[128,2048]{1,0:T(8,128)(2,1)S(1)}, u32[]{:S(2)}, u32[]{:S(2)}) collective-permute-start(bf16[128,2048]{1,0:T(8,128)(2,1)} %get-tuple-element.201), channel_id=1, source_target_pairs={{0,2},{1,3},{2,0},{3,1},{4,6},{5,7},{6,4},{7,5},{8,10},{9,11},{10,... | collective-permute-start | bytes 1572872 | tf_op jit(solution)/shard_map/ppermute | solution.py:330
  55.6 26.4 %collective-permute-start.94 = (bf16[128,2048]{1,0:T(8,128)(2,1)}, bf16[128,2048]{1,0:T(8,128)(2,1)S(1)}, u32[]{:S(2)}, u32[]{:S(2)}) collective-permute-start(bf16[128,2048]{1,0:T(8,128)(2,1)} %get-tuple-element.202), channel_id=1, source_target_pairs={{0,1},{1,2},{2,3},{3,0},{4,5},{5,6},{6,7},{7,4},{8,9},{9,10},{10,1... | collective-permute-start | bytes 1572872 | tf_op jit(solution)/shard_map/ppermute | solution.py:330
  55.6 26.3 %collective-permute-start.95 = (bf16[128,2048]{1,0:T(8,128)(2,1)}, bf16[128,2048]{1,0:T(8,128)(2,1)S(1)}, u32[]{:S(2)}, u32[]{:S(2)}) collective-permute-start(bf16[128,2048]{1,0:T(8,128)(2,1)} %get-tuple-element.203), channel_id=1, source_target_pairs={{0,3},{1,0},{2,1},{3,2},{4,7},{5,4},{6,5},{7,6},{8,11},{9,8},{10,9... | collective-permute-start | bytes 1572872 | tf_op jit(solution)/shard_map/ppermute | solution.py:330
  70.1 11.8 %copy-start = (bf16[128,2048]{1,0:T(8,128)(2,1)}, bf16[128,2048]{1,0:T(8,128)(2,1)S(1)}, u32[]{:S(2)}) copy-start(bf16[128,2048]{1,0:T(8,128)(2,1)S(1)} %collective-permute-done.93.r1_ref) | copy-start | bytes 1572868
  81.9 0.8 copy-start.1
  81.9 1.0 copy-start.2
  88.8 63.2 %all-to-all-start.2 = ((bf16[128,8,2048]{2,1,0:T(8,128)(2,1)}), bf16[128,8,2048]{2,1,0:T(8,128)(2,1)}, u32[]{:S(2)}, u32[]{:S(2)}) async-start(bf16[128,8,2048]{2,1,0:T(8,128)(2,1)} %bitcast.21), calls=%async_computation.2 | async-start | bytes 8388608 | tf_op jit(solution)/shard_map/all_to_all | solution.py:334
  152.1 57.3 %all-to-all-start = ((bf16[128,8,2048]{2,1,0:T(8,128)(2,1)}), bf16[128,8,2048]{2,1,0:T(8,128)(2,1)}, u32[]{:S(2)}, u32[]{:S(2)}) async-start(bf16[128,8,2048]{2,1,0:T(8,128)(2,1)} %bitcast.20), calls=%async_computation | async-start | bytes 8388608 | tf_op jit(solution)/shard_map/all_to_all | solution.py:334
  209.4 57.3 %all-to-all-start.3 = ((bf16[128,8,2048]{2,1,0:T(8,128)(2,1)}), bf16[128,8,2048]{2,1,0:T(8,128)(2,1)}, u32[]{:S(2)}, u32[]{:S(2)}) async-start(bf16[128,8,2048]{2,1,0:T(8,128)(2,1)} %bitcast.19), calls=%async_computation.3 | async-start | bytes 8388608 | tf_op jit(solution)/shard_map/all_to_all | solution.py:334
  266.8 57.3 %all-to-all-start.1 = ((bf16[128,8,2048]{2,1,0:T(8,128)(2,1)}), bf16[128,8,2048]{2,1,0:T(8,128)(2,1)}, u32[]{:S(2)}, u32[]{:S(2)}) async-start(bf16[128,8,2048]{2,1,0:T(8,128)(2,1)} %bitcast.18), calls=%async_computation.1 | async-start | bytes 8388608 | tf_op jit(solution)/shard_map/all_to_all | solution.py:334

commit v4 on v3

--- a/solution.py
+++ b/solution.py
@@ -15,7 +15,6 @@
 DIST = 3
 CAP = 16
 CHUNKS = 2
-PAIR = 2
 ALL = ("ctx", "head")
 BF16 = jnp.bfloat16
 F32 = jnp.float32
@@ -32,14 +31,17 @@
 
 
 def attention_kernel(
-    place, wanted, q_ref, k_ref, v_ref, far0_ref, far1_ref, far2_ref, w_ref, *refs
+    place, wanted, q_ref, k_ref, v_ref, far0_ref, far1_ref, far2_ref, weight_ref, *refs
 ):
-    out_refs, mixed_ref = refs[:-1], refs[-1]
+    out_refs, (mixed_ref, w_ref, sem) = refs[:-3], refs[-3:]
     step = pl.program_id(0)
+    steps = len(out_refs)
     blocks = k_ref.shape[0] // BLK
     heads = q_ref.shape[1] // HD
-    block = lax.rem(place[0] + step, blocks)
+    block = place[1 + step]
     far_refs = (far0_ref, far1_ref, far2_ref)
+    load = pltpu.make_async_copy(weight_ref, w_ref, sem)
+    pl.when(step == 0)(load.start)
 
     def attend(at):
         near = at * BLK
@@ -47,47 +49,44 @@
             jnp.int32, (BLK, BLK), 1
         )
         bias = jnp.where(later, -jnp.inf, 0.0)
-        bias = jnp.concatenate([bias] * PAIR, axis=1)
-        reach = [jnp.where(place[1] >= wanted[0, j], 0.0, -jnp.inf) for j in range(DIST)]
+        bias = jnp.concatenate([bias] * heads, axis=1)
+        reach = [jnp.where(place[0] >= wanted[0, j], 0.0, -jnp.inf) for j in range(DIST)]
         keys = jnp.concatenate([k_ref[: near + BLK]] + [r[0] for r in far_refs], axis=0)
         values = jnp.concatenate([v_ref[: near + BLK]] + [r[1] for r in far_refs], axis=0)
-        for n in range(0, heads, PAIR):
-            query = jnp.concatenate(
-                [q_ref[:, (n + i) * HD : (n + i + 1) * HD] for i in range(PAIR)], axis=0
+        query = jnp.concatenate([q_ref[:, n * HD : (n + 1) * HD] for n in range(heads)], axis=0)
+        score = lax.dot_general(keys, query, NT, preferred_element_type=F32)
+        parts = [score[:near]] if at else []
+        parts.append(score[near : near + BLK] + bias)
+        for j in range(DIST):
+            start = near + (j + 1) * BLK
+            parts.append(score[start : start + BLK] + reach[j])
+        score = jnp.concatenate(parts, axis=0)
+        highest = jnp.max(score, axis=0, keepdims=True)
+        weight = jnp.exp2((score - highest) * EXPONENT)
+        denominator = jnp.sum(weight, axis=0, keepdims=True)
+        mixed = lax.dot_general(values, weight.astype(BF16), TN, preferred_element_type=F32)
+        mixed = mixed / denominator
+        for n in range(heads):
+            mixed_ref[pl.ds(step * BLK, BLK), n * HD : (n + 1) * HD] = (
+                mixed[:, n * BLK : (n + 1) * BLK].T.astype(BF16)
             )
-            score = lax.dot_general(keys, query, NT, preferred_element_type=F32)
-            parts = [score[:near]] if at else []
-            parts.append(score[near : near + BLK] + bias)
-            for j in range(DIST):
-                start = near + (j + 1) * BLK
-                parts.append(score[start : start + BLK] + reach[j])
-            score = jnp.concatenate(parts, axis=0)
-            highest = jnp.max(score, axis=0, keepdims=True)
-            weight = jnp.exp2((score - highest) * EXPONENT)
-            denominator = jnp.sum(weight, axis=0, keepdims=True)
-            mixed = lax.dot_general(values, weight.astype(BF16), TN, preferred_element_type=F32)
-            mixed = mixed / denominator
-            for i in range(PAIR):
-                mixed_ref[pl.ds(step * BLK, BLK), (n + i) * HD : (n + i + 1) * HD] = (
-                    mixed[:, i * BLK : (i + 1) * BLK].T.astype(BF16)
-                )
 
     for at in range(blocks):
         pl.when(block == at)(functools.partial(attend, at))
 
-    @pl.when(step == blocks - 1)
-    def _():
+    @pl.when(step == steps - 1)
+    def _():
+        load.wait()
         for i, out_ref in enumerate(out_refs):
             out_ref[...] = jnp.dot(
                 mixed_ref[i * BLK : (i + 1) * BLK], w_ref[...], preferred_element_type=F32
             ).astype(BF16)
 
 
-def attention(place, wanted, queries, keys, values, far, out_weight):
-    length, wide = queries.shape
+def attention(place, wanted, queries, keys, values, far, out_weight, steps):
+    wide = queries.shape[1]
     width = out_weight.shape[1]
-    blocks = length // BLK
-    at = lambda i, place: lax.rem(place[0] + i, blocks)
+    at = lambda i, place: place[1 + i]
     whole = lambda shape: pl.BlockSpec(
         shape, lambda i, p, w: (0,) * len(shape), pipeline_mode=pl.Buffered(1)
     )
@@ -95,18 +94,22 @@
         attention_kernel,
         grid_spec=pltpu.PrefetchScalarGridSpec(
             num_scalar_prefetch=2,
-            grid=(blocks,),
+            grid=(steps,),
             in_specs=[
                 pl.BlockSpec((BLK, wide), lambda i, p, w: (at(i, p), 0)),
                 whole(keys.shape),
                 whole(values.shape),
             ]
             + [pl.BlockSpec((2, BLK, HD), lambda i, p, w: (0, at(i, p), 0))] * DIST
-            + [whole(out_weight.shape)],
-            out_specs=(whole((BLK, width)),) * blocks,
-            scratch_shapes=[pltpu.VMEM((length, wide), BF16)],
-        ),
-        out_shape=(jax.ShapeDtypeStruct((BLK, width), BF16),) * blocks,
+            + [pl.BlockSpec(memory_space=pl.ANY)],
+            out_specs=(whole((BLK, width)),) * steps,
+            scratch_shapes=[
+                pltpu.VMEM((steps * BLK, wide), BF16),
+                pltpu.VMEM(out_weight.shape, BF16),
+                pltpu.SemaphoreType.DMA,
+            ],
+        ),
+        out_shape=(jax.ShapeDtypeStruct((BLK, width), BF16),) * steps,
         compiler_params=params(),
         name="attention",
     )(place, wanted, queries, keys, values, *far, out_weight)
@@ -178,7 +181,7 @@
 def norm_dispatch(own, others, residual, gain, send):
     tokens, width = residual.shape
     rows = send.shape[1]
-    step = 256
+    step = 512
     whole = lambda shape: pl.BlockSpec(shape, lambda i: (0,) * len(shape))
     return pl.pallas_call(
         norm_kernel,
@@ -207,7 +210,7 @@
 def dispatch(send, normed, chunk):
     tokens, width = normed.shape
     rows = send.shape[1]
-    step = 256
+    step = 512
     return pl.pallas_call(
         dispatch_kernel,
         grid=(rows // step,),
@@ -273,7 +276,7 @@
 def combine(table, rows, before, dtype, chunk):
     count, width = rows.shape
     tokens = table.shape[2] // 2
-    step = 256
+    step = 512
     whole = lambda shape: pl.BlockSpec(shape, lambda i: (0,) * len(shape))
     operands = (table, rows) + (() if before is None else (before,))
     return pl.pallas_call(
@@ -319,17 +322,24 @@
     tokens, width = residual.shape
     devices = lax.axis_size(ALL)
     me, head = lax.axis_index("ctx"), lax.axis_index("head")
-    place = jnp.stack([head, me])
     packed = jnp.stack([keys, values])
     far = [fetch(packed, distances[0, j]) for j in range(DIST)]
     send, table = tables(routes, route_weights, devices)
-    own, one, two, three = attention(
-        place, distances, queries, keys, values, far, out_weight
-    )
-    others = [
-        lax.ppermute(a, "head", [(i, (i + r) % 4) for i in range(4)])
-        for a, r in ((two, 2), (one, 1), (three, 3))
-    ]
+    group = lax.axis_size("head")
+
+    def project(*relative):
+        place = jnp.stack([me] + [lax.rem(head + r, group) for r in relative])
+        return attention(
+            place, distances, queries, keys, values, far, out_weight, len(relative)
+        )
+
+    def hand(block, by):
+        return lax.ppermute(block, "head", [(i, (i + by) % group) for i in range(group)])
+
+    (two,) = project(2)
+    two = hand(two, 2)
+    one, three, own = project(1, 3, 0)
+    others = [two, hand(one, 1), hand(three, 3)]
     attended, normed, first = norm_dispatch(own, others, residual, norm_gain, send)
     exchange = lambda a: lax.all_to_all(a, ALL, split_axis=0, concat_axis=0, tiled=True)
     arrived = [exchange(first)]

time: 334 us -> 321 us (0.961); the launches traced: 330 us -> 320 us
  waiting for transfers between devices: 204 us -> 192 us
  starting transfers between devices: 46.4 us -> 53.3 us
  Pallas kernels: 72.7 us -> 67.6 us
    ppermute x3, waiting for transfers between devices: 19.6 us -> 9.53 us  [hand(): lax.ppermute(block, 'head', [(i, (i + by) % group) for i in range(group)])]
    all_to_all x4, starting transfers between devices: 24.6 us -> 29.8 us  [body(): lax.all_to_all(a, ALL, split_axis=0, concat_axis=0, tiled=True)]
    pallas_call x1 -> x2, Pallas kernels: 16.1 us -> 14.4 us  [attention(): pl.pallas_call(attention_kernel, grid_spec=pltpu.PrefetchScalarGridSpec(n...]
  transfers between devices with their start and end apart: 10 -> 10, of which waited for: 9 -> 9; matrix products, arithmetic and copies ran while one was open for 0% -> 0% of each run, Pallas kernels for 14% -> 16%
where the time goes in v4:
time: 321 us; the launch traced here: 320 us
  waiting for transfers between devices  192 us (60%)
  Pallas kernels  67.6 us (21%)
  starting transfers between devices  53.3 us (17%)
    all_to_all x4, waiting for transfers between devices, body(): lax.all_to_all(a, ALL, split_axis=0, concat_axis=0, tiled=True)  171 us
    pallas_call x2, Pallas kernels, expert(): pl.pallas_call(expert_kernel, grid=(rows // step,), in_specs=[pl.BlockSpe...  31.1 us
    all_to_all x4, starting transfers between devices, body(): lax.all_to_all(a, ALL, split_axis=0, concat_axis=0, tiled=True)  29.8 us
    ppermute x3, starting transfers between devices, back(): return lax.ppermute(block, 'ctx', [(i, i + by) for i in range(shards - by)])  18.7 us
    pallas_call x2, Pallas kernels, attention(): pl.pallas_call(attention_kernel, grid_spec=pltpu.PrefetchScalarGridSpec(n...  14.4 us
    ppermute x3, waiting for transfers between devices, back(): return lax.ppermute(block, 'ctx', [(i, i + by) for i in range(shards - by)])  11.5 us
    ppermute x3, waiting for transfers between devices, hand(): lax.ppermute(block, 'head', [(i, (i + by) % group) for i in range(group)])  9.53 us
    pallas_call x2, Pallas kernels, combine(): pl.pallas_call(combine_kernel, grid=(count // step,), in_specs=[pl.BlockS...  8.86 us
  transfers between devices with their start and end apart: 10, of which 9 were waited for; matrix products, arithmetic and copies ran while one was open for 0% of the time, Pallas kernels for 16%

profile of v4, /device:TPU:1, one launch (start us, length us, event | category | flops | bytes accessed | tf_op | source)
XLA Modules:
  0.0 320.1 jit_solution(6784297119529059362)
XLA Ops:
  0.6 1.4 fusion
  4.0 1.0 pad_maximum_fusion
  5.0 11.5 %conditional.5 = (bf16[2,512,128]{2,1,0:T(8,128)(2,1)}) conditional(s32[]{:T(128)} %bitcast.8, bf16[2,512,128]{2,1,0:T(8,128)(2,1)S(1)} %pad_maximum_fusion, bf16[2,512,128]{2,1,0:T(8,128)(2,1)S(1)} %pad_maximum_fusion, bf16[2,512,128]{2,1,0:T(8,128)(2,1)S(1)} %pad_maximum_fusion, ...), branch_computations={%region_62.0_spmd, %region_63.0_spmd, %region_64.0_spmd, %region_6... | conditional | bytes 1048624 | solution.py:304
  5.0 6.5 %collective-permute-start.66 = (bf16[2,512,128]{2,1,0:T(8,128)(2,1)S(1)}, bf16[2,512,128]{2,1,0:T(8,128)(2,1)}, u32[]{:S(2)}, u32[]{:S(2)}) collective-permute-start(bf16[2,512,128]{2,1,0:T(8,128)(2,1)S(1)} %param.66), channel_id=1, source_target_pairs={{0,20},{4,24},{8,28},{12,32},{16,36},{20,40},{24,44},{28,48},{32,5... | collective-permute-start | bytes 786440 | tf_op jit(solution)/shard_map/cond/branch_4_fun/ppermute | solution.py:302
  11.5 4.9 %collective-permute-done.66 = bf16[2,512,128]{2,1,0:T(8,128)(2,1)} collective-permute-done((bf16[2,512,128]{2,1,0:T(8,128)(2,1)S(1)}, bf16[2,512,128]{2,1,0:T(8,128)(2,1)}, u32[]{:S(2)}, u32[]{:S(2)}) %collective-permute-start.66) | collective-permute-done | bytes 262176 | tf_op jit(solution)/shard_map/cond/branch_4_fun/ppermute | solution.py:302
  16.4 9.0 %conditional.4 = (bf16[2,512,128]{2,1,0:T(8,128)(2,1)}) conditional(s32[]{:T(128)} %bitcast.7, bf16[2,512,128]{2,1,0:T(8,128)(2,1)S(1)} %pad_maximum_fusion, bf16[2,512,128]{2,1,0:T(8,128)(2,1)S(1)} %pad_maximum_fusion, bf16[2,512,128]{2,1,0:T(8,128)(2,1)S(1)} %pad_maximum_fusion, ...), branch_computations={%region_31.0_spmd, %region_32.0_spmd, %region_33.0_spmd, %region_3... | conditional | bytes 1048624 | solution.py:304
  16.4 5.3 %collective-permute-start.38 = (bf16[2,512,128]{2,1,0:T(8,128)(2,1)S(1)}, bf16[2,512,128]{2,1,0:T(8,128)(2,1)}, u32[]{:S(2)}, u32[]{:S(2)}) collective-permute-start(bf16[2,512,128]{2,1,0:T(8,128)(2,1)S(1)} %param.38), channel_id=1, source_target_pairs={{0,32},{4,36},{8,40},{12,44},{16,48},{20,52},{24,56},{28,60},{32,6... | collective-permute-start | bytes 786440 | tf_op jit(solution)/shard_map/cond/branch_7_fun/ppermute | solution.py:302
  21.8 3.7 %collective-permute-done.38 = bf16[2,512,128]{2,1,0:T(8,128)(2,1)} collective-permute-done((bf16[2,512,128]{2,1,0:T(8,128)(2,1)S(1)}, bf16[2,512,128]{2,1,0:T(8,128)(2,1)}, u32[]{:S(2)}, u32[]{:S(2)}) %collective-permute-start.38) | collective-permute-done | bytes 262176 | tf_op jit(solution)/shard_map/cond/branch_7_fun/ppermute | solution.py:302
  25.5 9.7 %conditional.3 = (bf16[2,512,128]{2,1,0:T(8,128)(2,1)}) conditional(s32[]{:T(128)} %bitcast.4, bf16[2,512,128]{2,1,0:T(8,128)(2,1)S(1)} %pad_maximum_fusion, bf16[2,512,128]{2,1,0:T(8,128)(2,1)S(1)} %pad_maximum_fusion, bf16[2,512,128]{2,1,0:T(8,128)(2,1)S(1)} %pad_maximum_fusion, ...), branch_computations={%region_0.0_spmd, %region_1.0_spmd, %region_2.0_spmd, %region_3.0_... | conditional | bytes 1048624 | solution.py:304
  25.5 6.9 %collective-permute-start.15 = (bf16[2,512,128]{2,1,0:T(8,128)(2,1)S(1)}, bf16[2,512,128]{2,1,0:T(8,128)(2,1)}, u32[]{:S(2)}, u32[]{:S(2)}) collective-permute-start(bf16[2,512,128]{2,1,0:T(8,128)(2,1)S(1)} %param.15), channel_id=1, source_target_pairs={{0,64},{4,68},{8,72},{12,76},{16,80},{20,84},{24,88},{28,92},{32,9... | collective-permute-start | bytes 786440 | tf_op jit(solution)/shard_map/cond/branch_15_fun/ppermute | solution.py:302
  32.4 2.8 collective-permute-done.15
  35.7 5.5 %attention.3 = bf16[128,2048]{1,0:T(8,128)(2,1)} custom-call(s32[2]{0:T(128)} %pad_add_fusion.1.place, s32[1,3]{1,0:T(1,128)} %wanted.3, bf16[512,1024]{1,0:T(8,128)(2,1)} %q_ref.3, bf16[512,128]{1,0:T(8,128)(2,1)} %k_ref.3, bf16[512,128]{1,0:T(8,128)(2,1)} %v_ref.3, bf16[2,512,128]{2,1,0:T(8,128)(2,1)} %get-tuple-element.210.far0_ref, ...), custom_call_target="tpu_custom_call" | custom-call | tf_op jit(solution)/shard_map/attention/pallas_call | solution.py:93
  41.2 1.0 collective-permute-start.93
  42.9 8.9 %attention.2 = (bf16[128,2048]{1,0:T(8,128)(2,1)}, bf16[128,2048]{1,0:T(8,128)(2,1)}, bf16[128,2048]{1,0:T(8,128)(2,1)}) custom-call(s32[4]{0:T(128)} %pad_add_fusion.place, s32[1,3]{1,0:T(1,128)} %wanted.3, bf16[512,1024]{1,0:T(8,128)(2,1)} %q_ref.3, bf16[512,128]{1,0:T(8,128)(2,1)} %k_ref.3, bf16[512,128]{1,0:T(8,128)(2,1)} %v_ref.3, ...), custom_call_target="tpu_custom_call" | custom-call | tf_op jit(solution)/shard_map/attention/pallas_call | solution.py:93
  51.8 3.5 %collective-permute-start.94 = (bf16[128,2048]{1,0:T(8,128)(2,1)}, bf16[128,2048]{1,0:T(8,128)(2,1)S(1)}, u32[]{:S(2)}, u32[]{:S(2)}) collective-permute-start(bf16[128,2048]{1,0:T(8,128)(2,1)} %get-tuple-element.200), channel_id=1, source_target_pairs={{0,1},{1,2},{2,3},{3,0},{4,5},{5,6},{6,7},{7,4},{8,9},{9,10},{10,1... | collective-permute-start | bytes 1572872 | tf_op jit(solution)/shard_map/ppermute | solution.py:337
  55.5 4.0 %tables.1 = (bf16[2,1024,128]{2,1,0:T(8,128)(2,1)}, bf16[2,1024,256]{2,1,0:T(8,128)(2,1)}) custom-call(s32[8,128]{1,0:T(8,128)} %bitcast.28, f32[8,128]{1,0:T(8,128)} %bitcast.29), custom_call_target="tpu_custom_call" | custom-call | tf_op jit(solution)/shard_map/tables/pallas_call | solution.py:152
  59.5 7.1 %collective-permute-done.94.r2_ref = bf16[128,2048]{1,0:T(8,128)(2,1)S(1)} collective-permute-done((bf16[128,2048]{1,0:T(8,128)(2,1)}, bf16[128,2048]{1,0:T(8,128)(2,1)S(1)}, u32[]{:S(2)}, u32[]{:S(2)}) %collective-permute-start.94) | collective-permute-done | bytes 524320 | tf_op jit(solution)/shard_map/ppermute | solution.py:337
  66.5 2.5 collective-permute-done.95.r3_ref
  69.8 5.4 %norm_dispatch.1 = (bf16[128,2048]{1,0:T(8,128)(2,1)}, bf16[128,2048]{1,0:T(8,128)(2,1)}, bf16[1024,2048]{1,0:T(8,128)(2,1)}) custom-call(bf16[128,2048]{1,0:T(8,128)(2,1)} %get-tuple-element.199.own_ref, bf16[128,2048]{1,0:T(8,128)(2,1)} %copy-done, bf16[128,2048]{1,0:T(8,128)(2,1)} %copy-done.1, bf16[128,2048]{1,0:T(8,128)(2,1)} %copy-done.2, ...), custom_call_target="tpu_custom_call" | custom-call | tf_op jit(solution)/shard_map/norm_dispatch/pallas_call | solution.py:186
  75.2 15.6 %all-to-all-start.2 = ((bf16[128,8,2048]{2,1,0:T(8,128)(2,1)}), bf16[128,8,2048]{2,1,0:T(8,128)(2,1)}, u32[]{:S(2)}, u32[]{:S(2)}) async-start(bf16[128,8,2048]{2,1,0:T(8,128)(2,1)} %bitcast.24), calls=%async_computation.2 | async-start | bytes 8388608 | tf_op jit(solution)/shard_map/all_to_all | solution.py:344
  90.8 3.9 %dispatch.1 = bf16[1024,2048]{1,0:T(8,128)(2,1)} custom-call(bf16[2,1024,128]{2,1,0:T(8,128)(2,1)} %get-tuple-element.202.send_ref, bf16[128,2048]{1,0:T(8,128)(2,1)} %get-tuple-element.205.normed_ref), custom_call_target="tpu_custom_call" | custom-call | tf_op jit(solution)/shard_map/dispatch/pallas_call | solution.py:214
  94.7 48.9 %all-to-all-done.2 = bf16[128,8,2048]{2,1,0:T(8,128)(2,1)} async-done(((bf16[128,8,2048]{2,1,0:T(8,128)(2,1)}), bf16[128,8,2048]{2,1,0:T(8,128)(2,1)}, u32[]{:S(2)}, u32[]{:S(2)}) %all-to-all-start.2) | async-done | bytes 4194336 | tf_op jit(solution)/shard_map/all_to_all | solution.py:344
  143.6 4.8 %all-to-all-start = ((bf16[128,8,2048]{2,1,0:T(8,128)(2,1)}), bf16[128,8,2048]{2,1,0:T(8,128)(2,1)}, u32[]{:S(2)}, u32[]{:S(2)}) async-start(bf16[128,8,2048]{2,1,0:T(8,128)(2,1)} %bitcast.23), calls=%async_computation | async-start | bytes 8388608 | tf_op jit(solution)/shard_map/all_to_all | solution.py:344
  148.4 15.5 %expert.3 = bf16[1024,2048]{1,0:T(8,128)(2,1)} custom-call(bf16[1024,2048]{1,0:T(8,128)(2,1)} %bitcast.18.x_ref, bf16[1,2048,1536]{2,1,0:T(8,128)(2,1)} %gate_up_ref.3, bf16[1,768,2048]{2,1,0:T(8,128)(2,1)} %down_ref.3), custom_call_target="tpu_custom_call" | custom-call | tf_op jit(solution)/shard_map/expert/pallas_call | solution.py:241
  163.9 37.0 %all-to-all-done = bf16[128,8,2048]{2,1,0:T(8,128)(2,1)} async-done(((bf16[128,8,2048]{2,1,0:T(8,128)(2,1)}), bf16[128,8,2048]{2,1,0:T(8,128)(2,1)}, u32[]{:S(2)}, u32[]{:S(2)}) %all-to-all-start) | async-done | bytes 4194336 | tf_op jit(solution)/shard_map/all_to_all | solution.py:344
  201.0 4.8 %all-to-all-start.3 = ((bf16[128,8,2048]{2,1,0:T(8,128)(2,1)}), bf16[128,8,2048]{2,1,0:T(8,128)(2,1)}, u32[]{:S(2)}, u32[]{:S(2)}) async-start(bf16[128,8,2048]{2,1,0:T(8,128)(2,1)} %bitcast.22), calls=%async_computation.3 | async-start | bytes 8388608 | tf_op jit(solution)/shard_map/all_to_all | solution.py:344
  205.7 15.5 %expert.2 = bf16[1024,2048]{1,0:T(8,128)(2,1)} custom-call(bf16[1024,2048]{1,0:T(8,128)(2,1)} %bitcast.14.x_ref, bf16[1,2048,1536]{2,1,0:T(8,128)(2,1)} %gate_up_ref.3, bf16[1,768,2048]{2,1,0:T(8,128)(2,1)} %down_ref.3), custom_call_target="tpu_custom_call" | custom-call | tf_op jit(solution)/shard_map/expert/pallas_call | solution.py:241
  221.3 37.1 %all-to-all-done.3 = bf16[128,8,2048]{2,1,0:T(8,128)(2,1)} async-done(((bf16[128,8,2048]{2,1,0:T(8,128)(2,1)}), bf16[128,8,2048]{2,1,0:T(8,128)(2,1)}, u32[]{:S(2)}, u32[]{:S(2)}) %all-to-all-start.3) | async-done | bytes 4194336 | tf_op jit(solution)/shard_map/all_to_all | solution.py:344
  258.3 4.8 %all-to-all-start.1 = ((bf16[128,8,2048]{2,1,0:T(8,128)(2,1)}), bf16[128,8,2048]{2,1,0:T(8,128)(2,1)}, u32[]{:S(2)}, u32[]{:S(2)}) async-start(bf16[128,8,2048]{2,1,0:T(8,128)(2,1)} %bitcast.21), calls=%async_computation.1 | async-start | bytes 8388608 | tf_op jit(solution)/shard_map/all_to_all | solution.py:344
  263.1 4.4 %combine.2.refs_0_ = f32[128,2048]{1,0:T(8,128)} custom-call(bf16[2,1024,256]{2,1,0:T(8,128)(2,1)} %get-tuple-element.204.table_ref, bf16[1024,2048]{1,0:T(8,128)(2,1)} %bitcast.20.rows_ref), custom_call_target="tpu_custom_call" | custom-call | tf_op jit(solution)/shard_map/combine/pallas_call | solution.py:282
  267.5 48.2 %all-to-all-done.1 = bf16[128,8,2048]{2,1,0:T(8,128)(2,1)} async-done(((bf16[128,8,2048]{2,1,0:T(8,128)(2,1)}), bf16[128,8,2048]{2,1,0:T(8,128)(2,1)}, u32[]{:S(2)}, u32[]{:S(2)}) %all-to-all-start.1) | async-done | bytes 4194336 | tf_op jit(solution)/shard_map/all_to_all | solution.py:344
  315.7 4.5 %combine.3 = bf16[128,2048]{1,0:T(8,128)(2,1)} custom-call(bf16[2,1024,256]{2,1,0:T(8,128)(2,1)} %get-tuple-element.204.table_ref, bf16[1024,2048]{1,0:T(8,128)(2,1)} %bitcast.16.rows_ref, f32[128,2048]{1,0:T(8,128)} %combine.2.refs_0_), custom_call_target="tpu_custom_call" | custom-call | tf_op jit(solution)/shard_map/combine/pallas_call | solution.py:282
  (10 shorter events, 2.2 us)
Async XLA Ops:
  5.0 11.4 %collective-permute-start.66 = (bf16[2,512,128]{2,1,0:T(8,128)(2,1)S(1)}, bf16[2,512,128]{2,1,0:T(8,128)(2,1)}, u32[]{:S(2)}, u32[]{:S(2)}) collective-permute-start(bf16[2,512,128]{2,1,0:T(8,128)(2,1)S(1)} %param.66), channel_id=1, source_target_pairs={{0,20},{4,24},{8,28},{12,32},{16,36},{20,40},{24,44},{28,48},{32,5... | collective-permute-start | bytes 786440 | tf_op jit(solution)/shard_map/cond/branch_4_fun/ppermute | solution.py:302
  16.4 9.0 %collective-permute-start.38 = (bf16[2,512,128]{2,1,0:T(8,128)(2,1)S(1)}, bf16[2,512,128]{2,1,0:T(8,128)(2,1)}, u32[]{:S(2)}, u32[]{:S(2)}) collective-permute-start(bf16[2,512,128]{2,1,0:T(8,128)(2,1)S(1)} %param.38), channel_id=1, source_target_pairs={{0,32},{4,36},{8,40},{12,44},{16,48},{20,52},{24,56},{28,60},{32,6... | collective-permute-start | bytes 786440 | tf_op jit(solution)/shard_map/cond/branch_7_fun/ppermute | solution.py:302
  25.5 9.7 %collective-permute-start.15 = (bf16[2,512,128]{2,1,0:T(8,128)(2,1)S(1)}, bf16[2,512,128]{2,1,0:T(8,128)(2,1)}, u32[]{:S(2)}, u32[]{:S(2)}) collective-permute-start(bf16[2,512,128]{2,1,0:T(8,128)(2,1)S(1)} %param.15), channel_id=1, source_target_pairs={{0,64},{4,68},{8,72},{12,76},{16,80},{20,84},{24,88},{28,92},{32,9... | collective-permute-start | bytes 786440 | tf_op jit(solution)/shard_map/cond/branch_15_fun/ppermute | solution.py:302
  41.2 18.2 %collective-permute-start.93 = (bf16[128,2048]{1,0:T(8,128)(2,1)}, bf16[128,2048]{1,0:T(8,128)(2,1)S(1)}, u32[]{:S(2)}, u32[]{:S(2)}) collective-permute-start(bf16[128,2048]{1,0:T(8,128)(2,1)} %attention.3), channel_id=1, source_target_pairs={{0,2},{1,3},{2,0},{3,1},{4,6},{5,7},{6,4},{7,5},{8,10},{9,11},{10,... | collective-permute-start | bytes 1572872 | tf_op jit(solution)/shard_map/ppermute | solution.py:337
  51.8 14.7 %collective-permute-start.94 = (bf16[128,2048]{1,0:T(8,128)(2,1)}, bf16[128,2048]{1,0:T(8,128)(2,1)S(1)}, u32[]{:S(2)}, u32[]{:S(2)}) collective-permute-start(bf16[128,2048]{1,0:T(8,128)(2,1)} %get-tuple-element.200), channel_id=1, source_target_pairs={{0,1},{1,2},{2,3},{3,0},{4,5},{5,6},{6,7},{7,4},{8,9},{9,10},{10,1... | collective-permute-start | bytes 1572872 | tf_op jit(solution)/shard_map/ppermute | solution.py:337
  55.3 13.6 %collective-permute-start.95 = (bf16[128,2048]{1,0:T(8,128)(2,1)}, bf16[128,2048]{1,0:T(8,128)(2,1)S(1)}, u32[]{:S(2)}, u32[]{:S(2)}) collective-permute-start(bf16[128,2048]{1,0:T(8,128)(2,1)} %get-tuple-element.201), channel_id=1, source_target_pairs={{0,3},{1,0},{2,1},{3,2},{4,7},{5,4},{6,5},{7,6},{8,11},{9,8},{10,9... | collective-permute-start | bytes 1572872 | tf_op jit(solution)/shard_map/ppermute | solution.py:337
  59.5 9.5 %copy-start = (bf16[128,2048]{1,0:T(8,128)(2,1)}, bf16[128,2048]{1,0:T(8,128)(2,1)S(1)}, u32[]{:S(2)}) copy-start(bf16[128,2048]{1,0:T(8,128)(2,1)S(1)} %collective-permute-done.93.r1_ref) | copy-start | bytes 1572868
  66.5 2.5 copy-start.1
  69.0 0.8 copy-start.2
  75.2 68.4 %all-to-all-start.2 = ((bf16[128,8,2048]{2,1,0:T(8,128)(2,1)}), bf16[128,8,2048]{2,1,0:T(8,128)(2,1)}, u32[]{:S(2)}, u32[]{:S(2)}) async-start(bf16[128,8,2048]{2,1,0:T(8,128)(2,1)} %bitcast.24), calls=%async_computation.2 | async-start | bytes 8388608 | tf_op jit(solution)/shard_map/all_to_all | solution.py:344
  143.6 57.3 %all-to-all-start = ((bf16[128,8,2048]{2,1,0:T(8,128)(2,1)}), bf16[128,8,2048]{2,1,0:T(8,128)(2,1)}, u32[]{:S(2)}, u32[]{:S(2)}) async-start(bf16[128,8,2048]{2,1,0:T(8,128)(2,1)} %bitcast.23), calls=%async_computation | async-start | bytes 8388608 | tf_op jit(solution)/shard_map/all_to_all | solution.py:344
  201.0 57.3 %all-to-all-start.3 = ((bf16[128,8,2048]{2,1,0:T(8,128)(2,1)}), bf16[128,8,2048]{2,1,0:T(8,128)(2,1)}, u32[]{:S(2)}, u32[]{:S(2)}) async-start(bf16[128,8,2048]{2,1,0:T(8,128)(2,1)} %bitcast.22), calls=%async_computation.3 | async-start | bytes 8388608 | tf_op jit(solution)/shard_map/all_to_all | solution.py:344
  258.3 57.3 %all-to-all-start.1 = ((bf16[128,8,2048]{2,1,0:T(8,128)(2,1)}), bf16[128,8,2048]{2,1,0:T(8,128)(2,1)}, u32[]{:S(2)}, u32[]{:S(2)}) async-start(bf16[128,8,2048]{2,1,0:T(8,128)(2,1)} %bitcast.21), calls=%async_computation.1 | async-start | bytes 8388608 | tf_op jit(solution)/shard_map/all_to_all | solution.py:344
